TPU v7x, 32 devices: a whole 2x2x4 slice. The times are simulated.
32 devices in a mesh: dp: 8 (over y, x, core), sp: 4 (over z).
Axes of the slice: x: 2, y: 2, z: 4, core: 2. Of those that a mesh axis runs over, the one named last changes fastest.
Arguments:
- inputs: bfloat16 [16, 2048, 768], P('dp', 'sp'), may hold values from -6 to 6
- out_grad: bfloat16 [16, 2048, 768], P('dp', 'sp'), may hold values from -6 to 6
- segment_ids: int32 [16, 2048], P('dp'), may hold values from 0 to 7, as said below
- positions: int32 [16, 2048], P('dp'), may hold values from 0 to 1023, as said below
- norm1_gain: bfloat16 [768], replicated, may hold values from 0.5 to 1.5
- norm1_bias: bfloat16 [768], replicated, may hold values from -1.75 to 1.75
- norm2_gain: bfloat16 [768], replicated, may hold values from 0.5 to 1.5
- norm2_bias: bfloat16 [768], replicated, may hold values from -1.75 to 1.75
- query_weight: bfloat16 [768, 768], replicated, may hold values from -0.21875 to 0.21875
- query_bias: bfloat16 [768], replicated, may hold values from -1.75 to 1.75
- key_weight: bfloat16 [768, 64], replicated, may hold values from -0.21875 to 0.21875
- key_bias: bfloat16 [16], replicated, may hold values from -1.75 to 1.75
- value_weight: bfloat16 [768, 64], replicated, may hold values from -0.21875 to 0.21875
- value_bias: bfloat16 [64], replicated, may hold values from -1.75 to 1.75
- output_weight: bfloat16 [768, 768], replicated, may hold values from -2.5 to 2.5
- output_bias: bfloat16 [768], replicated, may hold values from -1.75 to 1.75
- hidden_weight: bfloat16 [768, 3072], replicated, may hold values from -0.21875 to 0.21875
- hidden_bias: bfloat16 [3072], replicated, may hold values from -1.75 to 1.75
- down_weight: bfloat16 [3072, 768], replicated, may hold values from -0.109375 to 0.109375
- down_bias: bfloat16 [768], replicated, may hold values from -1.75 to 1.75
Outputs:
- layer_out: bfloat16 [16, 2048, 768], P('dp', 'sp')
- input_grad: float32 [16, 2048, 768], P('dp', 'sp')
- norm1_gain_grad: float32 [768], P('sp')
- norm1_bias_grad: float32 [768], P('sp')
- norm2_gain_grad: float32 [768], P('sp')
- norm2_bias_grad: float32 [768], P('sp')
- query_weight_grad: float32 [768, 768], P('sp')
- query_bias_grad: float32 [768], P('sp')
- key_weight_grad: float32 [768, 64], P('sp')
- key_bias_grad: float32 [16], P('sp')
- value_weight_grad: float32 [768, 64], P('sp')
- value_bias_grad: float32 [64], P('sp')
- output_weight_grad: float32 [768, 768], P('sp')
- output_bias_grad: float32 [768], P('sp')
- hidden_weight_grad: float32 [768, 3072], P('sp')
- hidden_bias_grad: float32 [3072], P('sp')
- down_weight_grad: float32 [3072, 768], P('sp')
- down_bias_grad: float32 [768], P('sp')
Inputs may be any that keep to these rules, and one draw needn't show every extreme that they name: `segment_ids`: document numbers of a row start at 0 and rise by one at each of its 7 boundaries, so every row holds exactly 8 documents; the first document of every row holds exactly 1024 tokens and each other document fewer. `positions`: each token's place counted from 0 at the first token of its document.
All inputs are finite; a program needn't handle non-finite values.
Results may differ from a plain program's by a relative error of at most 0.0085.
The roundings to bfloat16 on the way count: a program that leaves them out, or rounds other values in their place, can miss the bound.
Values may be sent and summed in bfloat16 or wider, within the bound.
No kernel may reach another device: no remote copies, remote signals or barrier semaphores. Data moves between devices by JAX's collectives and lax.ppermute only.
A program may use at most 256 MiB of HBM per device.

v0:
```python
import functools
import jax
import jax.numpy as jnp
from jax import lax
from jax.experimental import pallas as pl
from jax.experimental.pallas import tpu as pltpu
from jax.sharding import PartitionSpec as P
EPS=1e-5
VMEM_ALL=67043328
NN=(((1,),(0,)),((),()))
NT=(((1,),(1,)),((),()))
TN=(((0,),(0,)),((),()))
BF=jnp.bfloat16
F32=jnp.float32
NEG=-1e30
C1=0.7071067811865476
C2=0.3989422804014327
def dotf(a,b,dims=NN):
    return lax.dot_general(a,b,dims,preferred_element_type=F32)
def ln(xv):
    m=jnp.mean(xv,-1,keepdims=True); c=xv-m
    s=lax.rsqrt(jnp.mean(c*c,-1,keepdims=True)+EPS)
    return c*s,s
def cost(flops,bytes_):
    return pl.CostEstimate(flops=int(flops),bytes_accessed=int(bytes_),transcendentals=0)
def params(n,mb):
    return pltpu.CompilerParams(dimension_semantics=("arbitrary",)*n,vmem_limit_bytes=VMEM_ALL if mb is None else mb<<20)
ANY=pl.BlockSpec(memory_space=pl.ANY)
hs=jax.ShapeDtypeStruct
def whole(a):
    z=(0,)*len(a.shape)
    return pl.BlockSpec(a.shape,lambda *_: z)
def lane_iota(shape):
    return lax.broadcasted_iota(jnp.int32,shape,len(shape)-1)
V_G1,V_B1,V_G2,V_B2,V_Q,V_KV,V_O,V_D,V_H=range(9)
def table_kernel(*refs):
    *vs,kb_ref,vb_ref,hb_ref,out_ref=refs
    D=out_ref.shape[1]
    for k,ref in zip((V_G1,V_B1,V_G2,V_B2,V_Q,V_O,V_D),vs):
        out_ref[k:k+1,:]=ref[...].astype(F32).reshape(1,D)
    n=kb_ref.shape[0]; h=vb_ref.shape[0]
    out_ref[V_KV:V_KV+1,:]=jnp.zeros((1,D),F32)
    out_ref[V_KV:V_KV+1,:n]=kb_ref[...].astype(F32).reshape(1,n)
    out_ref[V_KV:V_KV+1,h:2*h]=vb_ref[...].astype(F32).reshape(1,h)
    for i in range(4):
        out_ref[V_H+i:V_H+i+1,:]=hb_ref[i*D:(i+1)*D].astype(F32).reshape(1,D)
def table(*vs):
    return pl.pallas_call(table_kernel,out_shape=hs((V_H+4,vs[0].shape[0]),F32),compiler_params=params(0,None),name="table")(*vs)
def rope_apply(v,C,S,sign):
    l=lane_iota(v.shape)&63
    sh=jnp.where(l<8,pltpu.roll(v,120,1),jnp.where(l<16,pltpu.roll(v,8,1),0.0))
    return v*C+S*sh if sign>0 else v*C-S*sh
def rope_kv(v,C,S,sign):
    l=lane_iota(v.shape)
    return rope_apply(v,jnp.where(l<64,C,1.0),jnp.where(l<64,S,0.0),sign)
def pre_kernel(x_ref,g_ref,cs_ref,wq_ref,wk_ref,wv_ref,wo_ref,vec_ref,q_ref,kv_ref,do_ref,tab_ref,ai_ref):
    B=x_ref.shape[0]
    row=lambda k: vec_ref[k:k+1,:]
    n,_=ln(x_ref[...].astype(F32))
    ai=(n*row(V_G1)+row(V_B1)).astype(BF)
    ai_ref[...]=ai.T
    t=cs_ref[...]
    t=jnp.concatenate([t,jnp.zeros((128-t.shape[0],B),F32)],0).T
    l=lane_iota((B,128))
    co=jnp.where(l<8,t,0.0)
    c2=co+pltpu.roll(co,8,1)
    C=c2+pltpu.roll(c2,64,1)+jnp.where((l&63)>=16,1.0,0.0)
    sb=jnp.where((l>=8)&(l<16),t,0.0)
    s2=sb-pltpu.roll(sb,120,1)
    S=s2+pltpu.roll(s2,64,1)
    tab_ref[:,:128]=C
    tab_ref[:,128:]=jnp.where(l==127,pltpu.roll(t,111,1),S)
    q=dotf(ai,wq_ref[...])+row(V_Q)
    do=dotf(g_ref[...],wo_ref[...],NT)
    for k in range(q.shape[1]//128):
        c=slice(k*128,k*128+128)
        q_ref[k]=(rope_apply(q[:,c],C,S,1)*0.125).astype(BF)
        do_ref[k]=do[:,c].astype(BF)
    kv=jnp.concatenate([dotf(ai,wk_ref[...],NT),dotf(ai,wv_ref[...],NT)],1)+row(V_KV)[:,:128]
    kv_ref[...]=rope_kv(kv,C,S,1).astype(BF)
def pre(x,g,cs,wq,wk,wv,wo,vec,B=256):
    N,D=x.shape; NP=D//128
    row=lambda w: pl.BlockSpec((B,w),lambda j:(j,0))
    pair=pl.BlockSpec((NP,B,128),lambda j:(0,j,0)); col=lambda h: pl.BlockSpec((h,B),lambda j:(0,j))
    return pl.pallas_call(pre_kernel,grid=(N//B,),
      in_specs=[row(D),row(D),col(cs.shape[0])]+[whole(a) for a in (wq,wk,wv,wo,vec)],
      out_specs=[pair,row(128),pair,row(256),col(D)],
      out_shape=[hs((NP,N,128),BF),hs((N,128),BF),hs((NP,N,128),BF),hs((N,256),F32),hs((D,N),BF)],
      cost_estimate=cost(4e9,1e7),compiler_params=params(1,None),name="pre")(x,g,cs,wq,wk,wv,wo,vec)
def mlp_kernel(last,rows,*refs):
    if last:
        (sc,x_ref,g_ref,wa_ref,wb_ref,va_ref,vb_ref,vec_ref,r2_ref,r1_ref,dbs_ref,_a,_g,
         keep_ref,send_ref,act_hbm,gp_hbm,db_ref,w1_ref,w2_ref,b_ref,act_ref,gp_ref,sem)=refs
        mi_ref=x_ref
    else:
        (sc,x_ref,g_ref,wa_ref,wb_ref,va_ref,vb_ref,vec_ref,
         out_ref,act_hbm,gp_hbm,db_ref,mi_ref,w1_ref,w2_ref,b_ref,act_ref,gp_ref,sem)=refs
    j=pl.program_id(0); N,D=x_ref.shape; W=wa_ref.shape[1]
    h=sc[0]
    def copies(jj):
        out=[]
        for i,(scr,hbm) in enumerate(((act_ref,act_hbm),(gp_ref,gp_hbm))):
            for k in (0,1):
                off=pl.multiple_of((2*(2*jj+k)+h)*W,W)
                out.append(pltpu.make_async_copy(scr.at[:,k*W:(k+1)*W],hbm.at[:,pl.ds(off,W)],sem.at[i,k]))
        return out
    if not last:
        @pl.when(j==0)
        def _():
            def body(i,_):
                r=pl.ds(pl.multiple_of(i*256,256),256)
                n,_s=ln(x_ref[r,:].astype(F32))
                mi_ref[r,:]=(n*vec_ref[V_G2:V_G2+1,:]+vec_ref[V_B2:V_B2+1,:]).astype(BF)
                return 0
            lax.fori_loop(0,N//256,body,0)
    w1_ref[:,:W]=wa_ref[...]; w1_ref[:,W:]=wb_ref[...]
    w2_ref[:W,:]=va_ref[...]; w2_ref[W:,:]=vb_ref[...]
    lane=pl.ds(pl.multiple_of(h*W,128),W)
    b_ref[:,:W]=vec_ref[pl.ds(V_H+2*j,1),lane]; b_ref[:,W:]=vec_ref[pl.ds(V_H+2*j+1,1),lane]
    @pl.when(j>0)
    def _():
        for c in copies(j-1): c.wait()
    for r in range(0,N,rows):
        sl=slice(r,r+rows)
        pre_=dotf(mi_ref[sl,:],w1_ref[...])+b_ref[...]
        da=dotf(g_ref[sl,:],w2_ref[...],NT)
        phi=0.5*(1.0+lax.erf(pre_*C1))
        act_ref[sl,:]=(pre_*phi).astype(BF)
        gp_ref[sl,:]=(da*(phi+pre_*(jnp.exp(pre_*pre_*-0.5)*C2))).astype(BF)
    for c in copies(j): c.start()
    db=jnp.sum(gp_ref[...].astype(F32),0,keepdims=True)
    if last:
        other=pl.ds(pl.multiple_of((1-h)*W,128),W)
        for k in (0,1):
            db_ref[pl.ds(2*j+k,1),lane]=db[:,k*W:(k+1)*W]
            db_ref[pl.ds(2*j+k,1),other]=dbs_ref[j][:,k*W:(k+1)*W]
    else: db_ref[0]=db
    q=D//4
    to=pl.ds(pl.multiple_of(j*q,q),q)
    if last: bit=sc[1]
    def part(i,_):
        c=pl.ds(pl.multiple_of(i*256,256),256)
        d2=dotf(act_ref[...],g_ref[:,c],TN).reshape(2,W,256)
        d1=dotf(mi_ref[...],gp_ref[:,c],TN).reshape(4,q,256)
        if last:
            d2=(d2+r2_ref[:,:,c].astype(F32)).astype(BF)
            d1=(d1+r1_ref[:,:,c].astype(F32)).astype(BF)
            @pl.when(bit==0)
            def _():
                keep_ref[pl.ds(2*j,2),:,c]=d2; send_ref[:,to,c]=d1
            @pl.when(bit!=0)
            def _():
                send_ref[pl.ds(2*j,2),:,c]=d2; keep_ref[:,to,c]=d1
        else:
            out_ref[pl.ds(2*j,2),:W,c]=d2.astype(BF)
            out_ref[:,pl.ds(pl.multiple_of(W+j*q,q),q),c]=d1.astype(BF)
        return 0
    lax.fori_loop(0,2*W//256,part,0)
    @pl.when(j==pl.num_programs(0)-1)
    def _():
        for c in copies(j): c.wait()
def mlp_half(sc,x,g,w1,w2,vec,recv=None,dbs=None,act=None,gp=None,rows=256):
    N,D=x.shape; F=w1.shape[1]; W=F//8
    last=recv is not None
    cb=lambda sh,k,ax: pl.BlockSpec(sh,(lambda j,s:(0,2*(2*j+k)+s[0])) if ax else (lambda j,s:(2*(2*j+k)+s[0],0)))
    ins=[whole(x),whole(g),cb((D,W),0,1),cb((D,W),1,1),cb((W,D),0,0),cb((W,D),1,0),whole(vec)]
    args=[x,g,w1,w1,w2,w2,vec]
    ag=[hs((N,F),BF),hs((N,F),BF),hs((2,1,2*W),F32)]
    ags=[ANY,ANY,pl.BlockSpec((1,1,2*W),lambda j,s:(j,0,0))]
    alias={}; scr=[]
    if last:
        ins+=[pl.BlockSpec((2,W,D),lambda j,s:(j,0,0)),pl.BlockSpec((4,D//4,D),lambda j,s:(0,W//(D//4)+j,0)),whole(dbs),ANY,ANY]
        args+=[recv,recv,dbs,act,gp]
        outs=[hs((4,W,D),BF)]*2+ag[:2]+[hs((4,2*W),F32)]
        ospec=[whole(outs[0])]*2+ags[:2]+[whole(outs[-1])]
        alias={1+10:2,1+11:3}
    else:
        outs=[hs((4,2*W,D),BF)]+ag+[hs((N,D),BF)]
        ospec=[whole(outs[0])]+ags+[whole(outs[-1])]
    return pl.pallas_call(functools.partial(mlp_kernel,last,rows),
        grid_spec=pltpu.PrefetchScalarGridSpec(num_scalar_prefetch=1,grid=(2,),in_specs=ins,out_specs=ospec,
            scratch_shapes=[pltpu.VMEM((D,2*W),BF),pltpu.VMEM((2*W,D),BF),pltpu.VMEM((1,2*W),F32),
                            pltpu.VMEM((N,2*W),BF),pltpu.VMEM((N,2*W),BF),pltpu.SemaphoreType.DMA((2,2))]),
        out_shape=outs,input_output_aliases=alias,cost_estimate=cost(4*N*D*F*1.3,20e6),
        compiler_params=params(1,None),name="mlp_keep" if last else "mlp_send")(sc,*args)

def attn_kernel(RB,q_ref,do_ref,kv_ref,kvp_ref,tab_ref,o_ref,dq_ref,dk_ref,dp_out,kx_ref,bias_ref,s_ref,d_ref,p_ref,ds_ref,acc_ref,qt_ref,oa_ref):
    step=pl.program_id(0)
    T=q_ref.shape[1]; QB=T//2
    @pl.when(step==0)
    def _():
        for i,ref in enumerate((kvp_ref,kv_ref)):
            kv=ref[...].astype(F32)
            l=lane_iota(kv.shape)
            ke=jnp.where(l<64,kv,0.0); vo=jnp.where(l>=64,kv,0.0)
            sl=slice(i*T,(i+1)*T)
            kx_ref[0,sl,:]=ke.astype(BF)
            kx_ref[1,sl,:]=pltpu.roll(ke,64,1).astype(BF)
            kx_ref[2,sl,:]=pltpu.roll(vo,64,1).astype(BF)
            kx_ref[3,sl,:]=vo.astype(BF)
        def mask(i,_):
            r=pl.ds(pl.multiple_of(i*64,64),64)
            kk=lane_iota((64,2*T))-T
            qi=lax.broadcasted_iota(jnp.int32,(64,2*T),0)+i*64
            ok=(kk.astype(F32)>=tab_ref[r,255:256])&(kk<=qi)
            bias_ref[r,:]=jnp.where(ok,0.0,NEG)
            return 0
        lax.fori_loop(0,T//64,mask,0)
        acc_ref[...]=jnp.zeros_like(acc_ref)
    def run(lo):
        units=[(qb,e) for qb in (0,1) for e in (0,1)]
        rng=lambda qb: (lo,T+(qb+1)*QB)
        def mm1(u):
            qb,e=units[u]; a,b=rng(qb); n=b-a; z=u%2; rs=slice(qb*QB,(qb+1)*QB)
            qs=q_ref[:,rs,:].reshape(2*QB,128); dv=do_ref[:,rs,:].reshape(2*QB,128)
            if e==0:
                qt_ref[0,qb]=qs.T; qt_ref[1,qb]=dv.T
            s_ref[z,:,:n]=dotf(qs,kx_ref[e,a:b,:],NT)
            d_ref[z,:,:n]=dotf(dv,kx_ref[2+e,a:b,:],NT)
        def vp(u):
            qb,e=units[u]; a,b=rng(qb); n=b-a; z=u%2
            for r in range(0,2*QB,RB):
                rr=slice(r,r+RB); br=qb*QB+r%QB
                s=s_ref[z,rr,:n]+bias_ref[br:br+RB,a:b]
                m=jnp.max(s,-1,keepdims=True)
                p=jnp.exp(s-m)
                p=p*(1.0/jnp.sum(p,-1,keepdims=True))
                p_ref[z,rr,:n]=p.astype(BF)
                t=p*d_ref[z,rr,:n]
                ds_ref[z,rr,:n]=(t-p*jnp.sum(t,-1,keepdims=True)).astype(BF)
        def mm2(u):
            qb,e=units[u]; a,b=rng(qb); n=b-a; z=u%2; rs=slice(qb*QB,(qb+1)*QB)
            pb=p_ref[z,:,:n]; dsb=ds_ref[z,:,:n]
            o=dotf(pb,kx_ref[2+e,a:b,:]); dq=dotf(dsb,kx_ref[e,a:b,:])
            h=slice(e*64,e*64+64)
            acc_ref[:64,a:b]+=dotf(qt_ref[0,qb,h,:],dsb)
            acc_ref[64:,a:b]+=dotf(qt_ref[1,qb,h,:],pb)
            if e==0:
                oa_ref[0]=o; oa_ref[1]=dq
            else:
                oo=(oa_ref[0]+o).astype(BF)
                dq=((oa_ref[1]+dq)*0.125)
                C=tab_ref[rs,:128]; S=tab_ref[rs,128:]
                for k in (0,1):
                    o_ref[rs,k*128:(k+1)*128]=oo[k*QB:(k+1)*QB]
                    dq_ref[rs,k*128:(k+1)*128]=rope_apply(dq[k*QB:(k+1)*QB],C,S,-1).astype(BF)
        mm1(0)
        mm1(1); vp(0)
        mm2(0); mm1(2); vp(1)
        mm2(1); mm1(3); vp(2)
        mm2(2); vp(3)
        mm2(3)
    run(0)
    @pl.when(step==pl.num_programs(0)-1)
    def _():
        dp_out[...]=acc_ref[:,:T].astype(BF)
        dk_ref[...]=acc_ref[:,T:]
def attn_row(row,q,do,kv,kvp,tab,prev=None,T=512,RB=32):
    NP,N,_=q.shape; QB=T//2
    bf=BF; f=F32
    hb=pl.BlockSpec((2,T,128),lambda h:(h,row,0)); rb=lambda w: pl.BlockSpec((T,w),lambda h:(row,0))
    def body(q_ref,do_ref,kv_ref,kvp_ref,tab_ref,*rest):
        if prev is not None: rest=rest[2:]
        attn_kernel(RB,q_ref,do_ref,kv_ref,kvp_ref,tab_ref,*rest)
    ins=[hb,hb,rb(128),rb(128),rb(256)]; args=[q,do,kv,kvp,tab]; alias={}
    if prev is not None:
        ins+=[ANY,ANY]; args+=list(prev); alias={5:0,6:1}
    c=lambda: pl.BlockSpec((128,T),lambda h:(0,0)); ob=pl.BlockSpec((T,256),lambda h:(row,h))
    return pl.pallas_call(body,
      grid=(NP//2,),in_specs=ins,out_specs=[ob,ob,c(),c()],
        scratch_shapes=[pltpu.VMEM((4,2*T,128),bf),pltpu.VMEM((T,2*T),f),pltpu.VMEM((2,2*QB,2*T),f),pltpu.VMEM((2,2*QB,2*T),f),
                        pltpu.VMEM((2,2*QB,2*T),bf),pltpu.VMEM((2,2*QB,2*T),bf),pltpu.VMEM((128,2*T),f),pltpu.VMEM((2,2,128,2*QB),bf),pltpu.VMEM((2,2*QB,128),f)],
      out_shape=[hs((N,NP*128),bf)]*2+[hs((128,T),f),hs((128,T),bf)],
      input_output_aliases=alias,cost_estimate=cost(2.4e10,4e6),
      compiler_params=params(1,28),name=f"attn{row}")(*args)
def wgrad_kernel(sc,g_ref,o_ref,dq_ref,ai_ref,keep_ref,send_ref,qb_ref,ot_ref,so_ref,sa_ref):
    N,D=o_ref.shape; hr=D//8
    def turn(i,_):
        r=pl.ds(pl.multiple_of(i*256,256),256); ot_ref[:,r]=o_ref[r,:].T
        return 0
    lax.fori_loop(0,N//256,turn,0)
    for i,c in enumerate((1-sc[0],sc[0])):
        def move(s,_):
            src=pl.ds(pl.multiple_of(s*2*hr+c*hr,hr),hr); to=pl.ds(pl.multiple_of((4*i+s)*hr,hr),hr)
            so_ref[to,:]=ot_ref[src,:]; sa_ref[to,:]=ai_ref[src,:]
            return 0
        lax.fori_loop(0,4,move,0)
    def part(i,_):
        c=pl.ds(pl.multiple_of(i*256,256),256)
        for k,(a,b) in enumerate(((so_ref,g_ref),(sa_ref,dq_ref))):
            w=dotf(a[...],b[:,c]).astype(BF).reshape(8,hr,256); to=pl.ds(pl.multiple_of(k*D+i*256,256),256)
            send_ref[:,:,to]=w[:4]; keep_ref[:,:,to]=w[4:]
        return 0
    lax.fori_loop(0,D//256,part,0)
    qb_ref[...]=jnp.sum(dq_ref[...].astype(F32),0,keepdims=True)
def wgrad(sc,g,o,dq,ai):
    N,D=g.shape
    args=(g,o,dq,ai)
    part=pl.BlockSpec((4,D//8,2*D),lambda j,s:(0,0,0)); out=hs((4,D//8,2*D+128),BF)
    return pl.pallas_call(wgrad_kernel,
        grid_spec=pltpu.PrefetchScalarGridSpec(num_scalar_prefetch=1,grid=(1,),in_specs=[whole(a) for a in args],out_specs=[part,part,pl.BlockSpec((1,D),lambda j,s:(0,0))],
            scratch_shapes=[pltpu.VMEM((D,N),BF)]*3),
        out_shape=[out,out,hs((1,D),F32)],cost_estimate=cost(2.6e9,9e6),compiler_params=params(1,30),name="wgrad")(sc,*args)
def kvgrad_kernel(sc,da_ref,db_ref,ra_ref,rb_ref,tab_ref,ai_ref,_k,_s,keep_ref,send_ref,dkv_ref,kvb_ref,w_ref):
    D,N=ai_ref.shape; T=N//2; hr=D//8
    for i,(ref,rr) in enumerate(((da_ref,ra_ref),(db_ref,rb_ref))):
        sl=slice(i*T,(i+1)*T)
        dkv_ref[sl,:]=rope_kv((ref[...]+rr[...].astype(F32)).T,tab_ref[sl,:128],tab_ref[sl,128:],-1).astype(BF)
    kvb_ref[...]=jnp.sum(dkv_ref[...].astype(F32),0,keepdims=True)
    w_ref[...]=dotf(ai_ref[...],dkv_ref[...])
    for dst,c in ((send_ref,1-sc[0]),(keep_ref,sc[0])):
        for s in range(4):
            dst[s]=w_ref[pl.ds(pl.multiple_of(s*2*hr+c*hr,hr),hr),:].astype(BF)
def kvgrad(sc,d0,d1,r0,r1,tab,ai,keep,send):
    D,N=ai.shape
    args=(d0,d1,r0,r1,tab,ai)
    col=pl.BlockSpec((4,D//8,128),lambda j,s:(0,0,2*D//128))
    outs=[hs(keep.shape,BF),hs(send.shape,BF),hs((N,128),BF),hs((1,128),F32)]
    return pl.pallas_call(kvgrad_kernel,
        grid_spec=pltpu.PrefetchScalarGridSpec(num_scalar_prefetch=1,grid=(1,),in_specs=[whole(a) for a in args]+[ANY,ANY],out_specs=[col,col,whole(outs[2]),whole(outs[3])],
            scratch_shapes=[pltpu.VMEM((D,128),F32)]),
        out_shape=outs,input_output_aliases={7:0,8:1},cost_estimate=cost(2e8,4e6),compiler_params=params(1,16),name="kvgrad")(sc,*args,keep,send)
def rows_of(w,B): return pl.BlockSpec((B,w),lambda j:(j,0))
def product_kernel(dims,a_ref,w_ref,out_ref):
    @pl.when(pl.program_id(0)==0)
    def _(): out_ref[...]=jnp.zeros_like(out_ref)
    out_ref[...]+=dotf(a_ref[...],w_ref[...],dims)
def product(a,w,across,name):
    N,F=a.shape; D=w.shape[0] if across else w.shape[1]
    ws=pl.BlockSpec((D,D),(lambda j:(0,j)) if across else (lambda j:(j,0)))
    return pl.pallas_call(functools.partial(product_kernel,NT if across else NN),grid=(F//D,),
      in_specs=[pl.BlockSpec((N,D),lambda j:(0,j)),ws],out_specs=pl.BlockSpec((N,D),lambda j:(0,0)),out_shape=hs((N,D),F32),
      cost_estimate=cost(4.8e9,1.4e7),compiler_params=params(1,None),name=name)(a,w)
def postb_kernel(x_ref,g_ref,dq_ref,dkv_ref,c2_ref,wq_ref,wk_ref,wv_ref,vec_ref,ig_ref,sm_ref):
    j=pl.program_id(0)
    @pl.when(j==0)
    def _(): sm_ref[...]=jnp.zeros_like(sm_ref)
    g=g_ref[...].astype(F32)
    n,s=ln(x_ref[...].astype(F32))
    dkv=dkv_ref[...]
    c1=dotf(dq_ref[...],wq_ref[...],NT)+dotf(dkv[:,:64],wk_ref[...])+dotf(dkv[:,64:],wv_ref[...])
    c2=c2_ref[...]
    u=c1*vec_ref[V_G1:V_G1+1,:]+c2*vec_ref[V_G2:V_G2+1,:]
    ig_ref[...]=g+s*(u-jnp.mean(u,-1,keepdims=True)-n*jnp.mean(u*n,-1,keepdims=True))
    for i,v in enumerate((c1*n,c1,c2*n,c2,g)):
        sm_ref[i:i+1,:]+=jnp.sum(v,0,keepdims=True)
def postb(x,g,dq,dkv,c2,wq,wk,wv,vec,B=256):
    N,D=x.shape
    return pl.pallas_call(postb_kernel,grid=(N//B,),
      in_specs=[rows_of(D,B)]*3+[rows_of(128,B),rows_of(D,B)]+[whole(a) for a in (wq,wk,wv,vec)],
      out_specs=[rows_of(D,B),pl.BlockSpec((8,D),lambda j:(0,0))],
      out_shape=[hs((N,D),F32),hs((8,D),F32)],
      cost_estimate=cost(2e9,1.2e7),compiler_params=params(1,None),name="postb")(x,g,dq,dkv,c2,wq,wk,wv,vec)
def posta_kernel(x_ref,o_ref,mb_ref,wo_ref,vec_ref,lo_ref):
    lo_ref[...]=(x_ref[...].astype(F32)+(dotf(o_ref[...],wo_ref[...])+vec_ref[V_O:V_O+1,:])+(mb_ref[...]+vec_ref[V_D:V_D+1,:])).astype(BF)
def posta(x,o,mb,wo,vec,B=256):
    N,D=x.shape
    return pl.pallas_call(posta_kernel,grid=(N//B,),
      in_specs=[rows_of(D,B)]*3+[whole(a) for a in (wo,vec)],
      out_specs=rows_of(D,B),out_shape=hs((N,D),BF),
      cost_estimate=cost(2e9,9e6),compiler_params=params(1,None),name="posta")(x,o,mb,wo,vec)
def final_kernel(sc,m_ref,mr_ref,a_ref,ar_ref,s_ref,sr_ref,w1_ref,w2_ref,wo_ref,wq_ref,wk_ref,wv_ref,
                 n1g_ref,n1b_ref,n2g_ref,n2b_ref,ob_ref,qb_ref,hb_ref,kb_ref,vb_ref,kv_ref):
    W=w2_ref.shape[0]//2; D=m_ref.shape[1]; q=D//4; hr=a_ref.shape[0]; pr=hr//4; mr=m_ref.shape[0]//4
    for r0,(m,a) in enumerate(((m_ref,a_ref),(mr_ref,ar_ref))):
        h=sc[0]^r0
        def piece(k,_):
            i=sc[2+2*r0]^(k>>1); j=sc[3+2*r0]^(k&1)
            src=pl.ds(pl.multiple_of(k*mr,mr),mr)
            @pl.when(i==0)
            def _(): w2_ref[pl.ds(pl.multiple_of(h*W+j*mr,mr),mr),:]=m[src,:].astype(F32)
            @pl.when(i!=0)
            def _():
                for c in (0,1):
                    w1_ref[:,pl.ds(pl.multiple_of((2*j+c)*2*W+h*W,W),W)]=m[src,c*W:(c+1)*W].astype(F32)
            return 0
        lax.fori_loop(0,4,piece,0)
        for k in range(4):
            i=sc[2+2*r0]^(k>>1); j=sc[3+2*r0]^(k&1)
            to=pl.ds(pl.multiple_of(h*hr+i*2*pr+j*pr,pr),pr)
            wo_ref[to,:]=a[k*pr:(k+1)*pr,:D].astype(F32)
            wq_ref[to,:]=a[k*pr:(k+1)*pr,D:2*D].astype(F32)
            kv_ref[to,:]=a[k*pr:(k+1)*pr,2*D:].astype(F32)
    keys=kv_ref[...].T
    wk_ref[...]=keys[:64]; wv_ref[...]=keys[64:]
    t=s_ref[...]+sr_ref[...]
    for s in range(4):
        @pl.when(sc[1]==s)
        def _():
            for k,ref in enumerate((n1g_ref,n1b_ref,n2g_ref,n2b_ref,ob_ref,qb_ref)):
                ref[...]=t[k:k+1,s*q:(s+1)*q].reshape(q)
            hb_ref[...]=t[6+s:7+s,:].reshape(D)
            n=kb_ref.shape[0]; kb_ref[...]=t[10:11,s*n:(s+1)*n].reshape(n)
            n=vb_ref.shape[0]; vb_ref[...]=t[10:11,64+s*n:64+(s+1)*n].reshape(n)
def final(sc,m,mr,a,ar,s,sr,F,rotd):
    D=m.shape[1]; f=F32; v=hs((D//4,),f)
    outs=[hs((D//4,F),f),hs((F//4,D),f),hs((D//4,D),f),hs((D//4,D),f),hs((64,D//4),f),hs((64,D//4),f)]+[v]*6+[hs((D,),f),hs((rotd//4,),f),hs((16,),f)]
    return pl.pallas_call(final_kernel,
        grid_spec=pltpu.PrefetchScalarGridSpec(num_scalar_prefetch=1,grid=(1,),in_specs=[whole(u) for u in (m,mr,a,ar,s,sr)],out_specs=[whole(u) for u in outs],
            scratch_shapes=[pltpu.VMEM((D//4,128),F32)]),
        out_shape=outs,cost_estimate=cost(1e6,9e6),compiler_params=params(1,24),name="final")(sc,m,mr,a,ar,s,sr)
def bits_of(n):
    return n.bit_length()-1
def after(xs,*deps):
    out=lax.optimization_barrier(tuple(xs)+tuple(deps))
    return out[:len(xs)]
def dp_stages():
    dp=lax.axis_size("dp"); nb=bits_of(dp); i=lax.axis_index("dp")
    core=i&1
    st=[(core,[(k,k^1) for k in range(dp)],core)]
    for t in range(1,nb):
        up,down=t,nb-t
        a,b=(i>>up)&1,(i>>down)&1
        st.append((jnp.where(core==0,a,b),[(k,k^((1<<up) if k%2==0 else (1<<down))) for k in range(dp)],jnp.where(core==0,b,a)))
    return st
def pick(G,bit,ax): return lax.dynamic_index_in_dim(G,bit,ax,keepdims=False)
def add(a,b): return (a.astype(F32)+b.astype(F32)).astype(a.dtype)
class Stream:
    def __init__(self,stages,at,send,keep):
        self.st=stages; self.at=at; self.send=send; self.keep=keep; self.left=len(stages)
    def go(self):
        n=len(self.st)
        if self.at<n: axis,pairs="dp",self.st[self.at][1]
        else: axis="sp"; pairs=[(k,k^(1<<(self.at-n))) for k in range(lax.axis_size("sp"))]
        self.recv=lax.ppermute(self.send,axis,pairs)
        return self.recv
    def land(self):
        k,r=self.keep,self.recv; self.at+=1
        n=len(self.st); s=lax.axis_index("sp")
        if self.at<n:
            split=lambda t: t.reshape(t.shape[0],2,t.shape[1]//2,t.shape[2]); bit=self.st[self.at][0]; ax=1
        elif self.at==n:
            split=lambda t: t.reshape(2,2,t.shape[1],t.shape[2]); bit=s&1; ax=1
        elif self.at==n+1:
            split=lambda t: t; bit=s>>1; ax=0
        else:
            self.own=add(k,r); self.left=n
            return
        k,r=split(k),split(r)
        self.send=add(pick(k,1-bit,ax),pick(r,1-bit,ax))
        self.keep=add(pick(k,bit,ax),pick(r,bit,ax))
    def gather_go(self):
        self.left-=1
        self.recv=lax.ppermute(self.own,"dp",self.st[self.left][1])
        return self.recv
    def gather_land(self):
        self.own=jnp.concatenate([self.own,self.recv],0)
    def settle(self,x,of):
        n=len(self.st)
        if n<=3: return x
        g=x.reshape((4,)+(2,)*(n-3)+(-1,x.shape[1]))
        for t in range(3,n): g=jnp.where(self.st[t][of]==0,g,jnp.flip(g,t-2))
        return g.reshape(x.shape)
def on_device(inputs,out_grad,segment_ids,positions,norm1_gain,norm1_bias,norm2_gain,norm2_bias,query_weight,query_bias,key_weight,key_bias,value_weight,value_bias,output_weight,output_bias,hidden_weight,hidden_bias,down_weight,down_bias):
    sp=lax.axis_size("sp"); s=lax.axis_index("sp")
    R,T,D=inputs.shape; hd=key_weight.shape[1]; rotd=key_bias.shape[0]
    F=hidden_weight.shape[1]
    N=R*T
    x=inputs.reshape(N,D); g=out_grad.reshape(N,D)
    vec=table(norm1_gain,norm1_bias,norm2_gain,norm2_bias,query_bias,output_bias,down_bias,key_bias,value_bias,hidden_bias)
    pos=lax.dynamic_slice_in_dim(positions,s*T,T,1)
    st=dp_stages(); core=st[0][0]; bit1=st[1][0]
    back=[(i+1,i) for i in range(0,sp,2)]
    Ms,act,gp,dbs,mi=mlp_half(jnp.stack([1-core,bit1]),x,g,hidden_weight,down_weight,vec)
    Mr=lax.ppermute(Ms,"dp",st[0][1])
    pf=pos.astype(F32).reshape(N)
    freq=10000.0**(-(jnp.arange(rotd//2,dtype=F32)*2.0)/rotd)
    ang=pf[None,:]*freq[:,None]
    ds=(jnp.arange(T,dtype=F32)[None,:]-pos.astype(F32)).reshape(1,N)
    cs=jnp.concatenate([jnp.cos(ang),jnp.sin(ang),ds,jnp.zeros((7,N),F32)],0)
    xq,=after([x],dbs)
    q,kv,do,tab,ai=pre(xq,g,cs,query_weight,key_weight.T,value_weight.T,output_weight,vec)
    kv,Mr=after([kv,Mr],q)
    kvp=lax.ppermute(kv,"sp",[(i,i+1) for i in range(0,sp,2)])
    mi,=after([mi],q)
    keep,send,act,gp,dbk=mlp_half(jnp.stack([core,bit1]),mi,g,hidden_weight,down_weight,vec,recv=Mr,dbs=dbs,act=act,gp=gp)
    M=Stream(st,1,send,keep)
    M.send,kvp=after([M.send,kvp],dbk)
    M.go()
    q,=after([q],dbk)
    o,dq,d0,k0=attn_row(0,q,do,kv,kvp,tab,T=T)
    M.recv,k0=after([M.recv,k0],dq)
    M.land()
    r0=lax.ppermute(k0,"sp",back); M.go()
    o,dq=after([o,dq],M.send,k0)
    o,dq,d1,k1=attn_row(1,q,do,kv,kvp,tab,prev=(o,dq),T=T)
    k1,M.recv,r0=after([k1,M.recv,r0],dq)
    r1=lax.ppermute(k1,"sp",back)
    while True:
        M.land()
        if M.at>=len(st): break
        M.go()
    o_,=after([o],M.send,k1)
    sc=core.reshape(1)
    wkeep,wsend,qb=wgrad(sc,g,o_,dq,ai)
    M.send,wkeep,wsend,r1=after([M.send,wkeep,wsend,r1],qb)
    M.send,=after([M.send],r1)
    M.go()
    r1,=after([r1],M.send)
    wkeep,wsend,dkv,kvb=kvgrad(sc,d0,d1,r0,r1,tab,ai,wkeep,wsend)
    A=Stream(st,0,wsend,wkeep)
    small=None
    todo=[("dp",p) for _,p,_o in st]+[("sp",[(i,i^(1<<k)) for i in range(sp)]) for k in range(bits_of(sp))]
    c2=mb=ig=lo=sm=None
    fill=["c2","ig","mb","lo"]
    held=1
    busy=True
    while True:
        rs=A.at<len(st)+2
        ag=not rs and A.left>1
        if not (rs or ag or busy or M.left>1 or len(todo)>1): break
        if rs: A.go(); moved=[A.send]
        elif ag: A.gather_go(); moved=[A.own]
        else: moved=[]
        if not busy:
            if M.at<len(st)+2: M.go(); busy=True; held=1; moved.append(M.send)
            elif M.left>1: moved.append(M.own); M.gather_go(); busy=True; held=0 if M.left>1 else 1
        sr=None
        if small is not None and len(todo)>1: axis,pairs=todo.pop(0); sr=lax.ppermute(small,axis,pairs); moved.append(small)
        deps=[]
        if fill:
            k=fill.pop(0)
            if k=="c2": gk,=after([gp],*moved); c2=product(gk,hidden_weight,True,"back"); deps=[c2]
            if k=="ig": xk,=after([x],*moved); ig,sm=postb(xk,g,dq,dkv,c2,query_weight,key_weight.T,value_weight.T,vec); deps=[ig]
            if k=="mb": ak,=after([act],*moved); mb=product(ak,down_weight,False,"down"); deps=[mb]
            if k=="lo": xk,=after([x],*moved); lo=posta(xk,o,mb,output_weight,vec); deps=[lo]
        lands=busy and held==0
        got=([A.recv] if rs or ag else [])+([M.recv] if lands else [])+([sr] if sr is not None else [])
        got=list(after(got,*deps))
        if rs or ag: A.recv=got.pop(0)
        if lands: M.recv=got.pop(0)
        if sr is not None: small=small+got.pop(0)
        if rs: A.land()
        elif ag: A.gather_land()
        if lands:
            busy=False
            if M.at<len(st)+2: M.land()
            else: M.gather_land()
        held-=1
        if small is None and ig is not None:
            small=jnp.concatenate([sm[:5],qb,dbk,jnp.pad(kvb,((0,5),(0,D-kvb.shape[1])))],0)
    Mr=lax.ppermute(M.own,"dp",st[0][1])
    Ar=lax.ppermute(A.own,"dp",st[0][1])
    axis,pairs=todo.pop(0)
    sr=lax.ppermute(small,axis,pairs)
    zero=jnp.zeros_like(core)
    where=jnp.stack([core,s]+[st[t][of] if len(st)>t else zero for of in (0,2) for t in (1,2)])
    rw1,rw2,ro,rq,rk,rv,n1g,n1b,n2g,n2b,ob,qbg,hb,kb,vb=final(where,M.settle(M.own,0),M.settle(Mr,2),A.settle(A.own,0),A.settle(Ar,2),small,sr,F,rotd)
    return (lo.reshape(R,T,D),ig.reshape(R,T,D),n1g,n1b,n2g,n2b,rq,qbg,rk.T,kb,rv.T,vb,ro,ob,rw1,hb,rw2,ob)
def solution(mesh):
    t=P("dp","sp",None); m=P("dp",None); w=P()
    v=P("sp"); v2=P("sp",None)
    return jax.shard_map(on_device,mesh=mesh,in_specs=(t,t,m,m)+(w,)*16,
        out_specs=(t,t,v,v,v,v,v2,v,v2,v,v2,v,v2,v,v2,v,v2,v),check_vma=False)
```

profile of v0, /device:TPU:0, one launch (start us, length us, event | category | flops | bytes accessed | tf_op | source)
XLA Modules:
  0.0 221.2 jit_solution(11698285066462387557)
XLA Ops:
  1.3 1.5 table.1.refs_7_.vec_ref
  2.8 20.4 %mlp_send.1 = (bf16[4,768,768]{2,1,0:T(8,128)(2,1)}, bf16[1024,3072]{1,0:T(8,128)(2,1)}, bf16[1024,3072]{1,0:T(8,128)(2,1)}, f32[2,1,768]{2,1,0:T(1,128)}, bf16[1024,768]{1,0:T(8,128)(2,1)}) custom-call(s32[2]{0:T(128)} %get-tuple-element.204.refs_0_, bf16[1024,768]{1,0:T(8,128)(2,1)} %bitcast.89, bf16[1024,768]{1,0:T(8,128)(2,1)} %bitcast.84, ...), custom_call_target="tpu_custom_call" | custom-call | flops 12562779136 | bytes 20000000 | tf_op jit(solution)/shard_map/mlp_send/pallas_call | solution.py:180
  26.1 9.1 %pre.1 = (bf16[6,1024,128]{2,1,0:T(8,128)(2,1)}, bf16[1024,128]{1,0:T(8,128)(2,1)}, bf16[6,1024,128]{2,1,0:T(8,128)(2,1)}, f32[1024,256]{1,0:T(8,128)}, bf16[768,1024]{1,0:T(8,128)(2,1)}) custom-call(bf16[1024,768]{1,0:T(8,128)(2,1)} %bitcast.90, bf16[1024,768]{1,0:T(8,128)(2,1)} %bitcast.85, f32[24,1024]{1,0:T(8,128)} %maximum_maximum_fusion.cs_ref, ...), custom_call_target="tpu_custom_call" | custom-call | flops 4000000000 | bytes 10000000 | tf_op jit(solution)/shard_map/pre/pallas_call | solution.py:85
  35.3 5.2 %collective-permute-start.1 = (bf16[1024,128]{1,0:T(8,128)(2,1)}, bf16[1024,128]{1,0:T(8,128)(2,1)}, u32[]{:S(2)}, u32[]{:S(2)}) collective-permute-start(bf16[1024,128]{1,0:T(8,128)(2,1)} %get-tuple-element.118.kv_ref), channel_id=1, source_target_pairs={{0,1},{2,3},{4,5},{6,7},{8,9},{10,11},{12,13},{14,15},{16,17},{18,... | collective-permute-start | bytes 786440 | tf_op jit(solution)/shard_map/ppermute | solution.py:474
  40.5 19.6 %mlp_keep.1 = (bf16[4,384,768]{2,1,0:T(8,128)(2,1)}, bf16[4,384,768]{2,1,0:T(8,128)(2,1)}, bf16[1024,3072]{1,0:T(8,128)(2,1)}, bf16[1024,3072]{1,0:T(8,128)(2,1)}, f32[4,768]{1,0:T(4,128)}) custom-call(s32[2]{0:T(128)} %get-tuple-element.205.refs_0_, bf16[1024,768]{1,0:T(8,128)(2,1)} %get-tuple-element.109.refs_1_, ...), custom_call_target="tpu_custom_call", output_to_operand_aliasing={{2}: (11, {}), {3}: (12, {})} | custom-call | flops 12562779136 | bytes 20000000 | tf_op jit(solution)/shard_map/mlp_keep/pallas_call | solution.py:180
  60.1 1.5 collective-permute-start.2
  66.6 23.3 %attn0.1 = (bf16[1024,768]{1,0:T(8,128)(2,1)S(1)}, bf16[1024,768]{1,0:T(8,128)(2,1)S(1)}, f32[128,512]{1,0:T(8,128)S(1)}, bf16[128,512]{1,0:T(8,128)(2,1)S(1)}) custom-call(bf16[6,1024,128]{2,1,0:T(8,128)(2,1)S(1)} %copy-done.11, bf16[6,1024,128]{2,1,0:T(8,128)(2,1)S(1)} %copy-done.13, bf16[1024,128]{1,0:T(8,128)(2,1)S(1)} %copy-done.10, ...), custom_call_target="tpu_custom_call" | custom-call | flops 24000000000 | bytes 4000000 | tf_op jit(solution)/shard_map/attn0/pallas_call | solution.py:269
  90.5 1.6 collective-permute-start.3
  93.4 22.9 %attn1.1 = (bf16[1024,768]{1,0:T(8,128)(2,1)S(1)}, bf16[1024,768]{1,0:T(8,128)(2,1)S(1)}, f32[128,512]{1,0:T(8,128)S(1)}, bf16[128,512]{1,0:T(8,128)(2,1)S(1)}) custom-call(bf16[6,1024,128]{2,1,0:T(8,128)(2,1)S(1)} %copy-done.12, bf16[6,1024,128]{2,1,0:T(8,128)(2,1)S(1)} %copy-done.14, ...), custom_call_target="tpu_custom_call", output_to_operand_aliasing={{0}: (5, {}), {1}: (6, {})} | custom-call | flops 24000000000 | bytes 4000000 | tf_op jit(solution)/shard_map/attn1/pallas_call | solution.py:269
  120.0 4.8 %wgrad.1 = (bf16[4,96,1664]{2,1,0:T(8,128)(2,1)S(1)}, bf16[4,96,1664]{2,1,0:T(8,128)(2,1)}, f32[1,768]{1,0:T(1,128)S(1)}) custom-call(s32[1]{0:T(128)} %bitcast.1.sc, bf16[1024,768]{1,0:T(8,128)(2,1)S(1)} %bitcast.88, bf16[1024,768]{1,0:T(8,128)(2,1)S(1)} %get-tuple-element.139.o_ref, bf16[1024,768]{1,0:T(8,128)(2,1)S(1)} %get-tuple-element.134.dq_ref, ...), custom_call_target="tpu_custom_call" | custom-call | flops 2600000000 | bytes 9000000 | tf_op jit(solution)/shard_map/wgrad/pallas_call | solution.py:300
  124.8 1.7 kvgrad.1
  128.7 9.7 %back.1.c2_ref = f32[1024,768]{1,0:T(8,128)} custom-call(bf16[1024,3072]{1,0:T(8,128)(2,1)} %get-tuple-element.153.a_ref, bf16[768,3072]{1,0:T(8,128)(2,1)} %w_ref.2), custom_call_target="tpu_custom_call" | custom-call | flops 4800000000 | bytes 14000000 | tf_op jit(solution)/shard_map/back/pallas_call | solution.py:331
  138.5 3.0 %add_convert_fusion.3 = (bf16[4,1,48,1664]{3,2,0,1:T(8,128)(2,1)}, bf16[4,48,1664]{2,1,0:T(8,128)(2,1)}) fusion(bf16[4,2,48,1664]{3,2,1,0:T(8,128)(2,1)} %bitcast.14, s32[]{:T(128)S(6)} %select_n.69, bf16[4,2,48,1664]{3,2,1,0:T(8,128)(2,1)} %bitcast.83, s32[]{:T(128)S(6)} %select_n.70), kind=kLoop, calls=%fused_computation.3 | loop fusion | flops 2555904 | bytes 3833864 | tf_op jit(solution)/shard_map/convert_element_type | solution.py:417
  142.2 2.6 %collective-permute-start.8 = (bf16[2,192,768]{2,1,0:T(8,128)(2,1)}, bf16[2,192,768]{2,1,0:T(8,128)(2,1)}, u32[]{:S(2)}, u32[]{:S(2)}) collective-permute-start(bf16[2,192,768]{2,1,0:T(8,128)(2,1)} %get-tuple-element.146), channel_id=1, source_target_pairs={{0,1},{1,0},{2,3},{3,2},{4,5},{5,4},{6,7},{7,6},{8,9},{9,8},{10,11... | collective-permute-start | bytes 1769480 | tf_op jit(solution)/shard_map/ppermute | solution.py:425
  144.8 8.3 %postb.1 = (f32[1024,768]{1,0:T(8,128)}, f32[8,768]{1,0:T(8,128)}) custom-call(bf16[1024,768]{1,0:T(8,128)(2,1)} %bitcast.91, bf16[1024,768]{1,0:T(8,128)(2,1)} %bitcast.87, bf16[1024,768]{1,0:T(8,128)(2,1)} %copy-done.2, bf16[1024,128]{1,0:T(8,128)(2,1)} %copy-done.7, f32[1024,768]{1,0:T(8,128)} %back.1.c2_ref, bf16[768,768]{1,0:T(8,128)(2,1)} %wq_ref.3, ...), custom_call_target="tpu_custom_call" | custom-call | flops 2000000000 | bytes 12000000 | tf_op jit(solution)/shard_map/postb/pallas_call | solution.py:349
  153.1 1.5 select_maximum_fusion
  154.6 4.1 %collective-permute-done.8 = bf16[2,192,768]{2,1,0:T(8,128)(2,1)} collective-permute-done((bf16[2,192,768]{2,1,0:T(8,128)(2,1)}, bf16[2,192,768]{2,1,0:T(8,128)(2,1)}, u32[]{:S(2)}, u32[]{:S(2)}) %collective-permute-start.8) | collective-permute-done | bytes 589856 | tf_op jit(solution)/shard_map/ppermute | solution.py:425
  158.7 2.2 %add_convert_fusion.7 = (bf16[4,1,24,1664]{3,2,1,0:T(8,128)(2,1)}, bf16[4,24,1664]{2,1,0:T(8,128)(2,1)}) fusion(bf16[4,2,24,1664]{3,2,1,0:T(8,128)(2,1)} %bitcast.17, s32[]{:T(128)S(6)} %select_n.67, bf16[4,2,24,1664]{3,2,1,0:T(8,128)(2,1)} %bitcast.94, s32[]{:T(128)S(6)} %select_n.66), kind=kLoop, calls=%fused_computation.10 | loop fusion | flops 1277952 | bytes 1916936 | tf_op jit(solution)/shard_map/convert_element_type | solution.py:417
  161.8 1.7 fusion.7
  163.5 2.6 %collective-permute-start.12 = (bf16[192,768]{1,0:T(8,128)(2,1)}, bf16[192,768]{1,0:T(8,128)(2,1)}, u32[]{:S(2)}, u32[]{:S(2)}) collective-permute-start(bf16[192,768]{1,0:T(8,128)(2,1)} %fusion.7), channel_id=1, source_target_pairs={{0,2},{1,3},{2,0},{3,1},{4,6},{5,7},{6,4},{7,5},{8,10},{9,11},{10,... | collective-permute-start | bytes 884744 | tf_op jit(solution)/shard_map/ppermute | solution.py:425
  166.2 9.7 %down.1.mb_ref = f32[1024,768]{1,0:T(8,128)} custom-call(bf16[1024,3072]{1,0:T(8,128)(2,1)} %get-tuple-element.163.a_ref, bf16[3072,768]{1,0:T(8,128)(2,1)} %w_ref.3), custom_call_target="tpu_custom_call" | custom-call | flops 4800000000 | bytes 14000000 | tf_op jit(solution)/shard_map/down/pallas_call | solution.py:331
  175.9 2.0 add_convert_fusion.8
  177.8 1.5 fusion.17
  179.3 2.2 collective-permute-start.11
  182.4 5.9 %posta.1 = bf16[1024,768]{1,0:T(8,128)(2,1)} custom-call(bf16[1024,768]{1,0:T(8,128)(2,1)} %bitcast.92, bf16[1024,768]{1,0:T(8,128)(2,1)} %copy-done.4, f32[1024,768]{1,0:T(8,128)} %down.1.mb_ref, bf16[768,768]{1,0:T(8,128)(2,1)} %wo_ref.3, f32[12,768]{1,0:T(8,128)} %table.1.refs_7_.vec_ref), custom_call_target="tpu_custom_call" | custom-call | flops 2000000000 | bytes 9000000 | tf_op jit(solution)/shard_map/posta/pallas_call | solution.py:358
  192.3 1.5 collective-permute-start.16
  193.8 3.1 %collective-permute-done.16 = f32[16,768]{1,0:T(8,128)S(1)} collective-permute-done((f32[16,768]{1,0:T(8,128)S(1)}, f32[16,768]{1,0:T(8,128)S(1)}, u32[]{:S(2)}, u32[]{:S(2)}) %collective-permute-start.16) | collective-permute-done | bytes 49184 | tf_op jit(solution)/shard_map/ppermute | solution.py:519
  200.6 4.1 %collective-permute-done.18 = f32[16,768]{1,0:T(8,128)S(1)} collective-permute-done((f32[16,768]{1,0:T(8,128)S(1)}, f32[16,768]{1,0:T(8,128)S(1)}, u32[]{:S(2)}, u32[]{:S(2)}) %collective-permute-start.18) | collective-permute-done | bytes 49184 | tf_op jit(solution)/shard_map/ppermute | solution.py:519
  205.9 4.2 %collective-permute-done.19 = bf16[48,1664]{1,0:T(8,128)(2,1)S(1)} collective-permute-done((bf16[48,1664]{1,0:T(8,128)(2,1)S(1)}, bf16[48,1664]{1,0:T(8,128)(2,1)S(1)}, u32[]{:S(2)}, u32[]{:S(2)}) %collective-permute-start.19) | collective-permute-done | bytes 159776 | tf_op jit(solution)/shard_map/ppermute | solution.py:444
  210.9 2.6 %collective-permute-start.23 = (f32[16,768]{1,0:T(8,128)S(1)}, f32[16,768]{1,0:T(8,128)S(1)}, u32[]{:S(2)}, u32[]{:S(2)}) collective-permute-start(f32[16,768]{1,0:T(8,128)S(1)} %add.165.s_ref), channel_id=1, source_target_pairs={{0,2},{1,3},{2,0},{3,1},{4,6},{5,7},{6,4},{7,5},{8,10},{9,11},{10,... | collective-permute-start | bytes 147464 | tf_op jit(solution)/shard_map/ppermute | solution.py:545
  213.6 2.5 %collective-permute-done.23.sr_ref = f32[16,768]{1,0:T(8,128)S(1)} collective-permute-done((f32[16,768]{1,0:T(8,128)S(1)}, f32[16,768]{1,0:T(8,128)S(1)}, u32[]{:S(2)}, u32[]{:S(2)}) %collective-permute-start.23) | collective-permute-done | bytes 49184 | tf_op jit(solution)/shard_map/ppermute | solution.py:545
  216.1 3.9 %final.1 = (f32[192,3072]{1,0:T(8,128)}, f32[768,768]{1,0:T(8,128)}, f32[192,768]{1,0:T(8,128)}, f32[192,768]{1,0:T(8,128)}, f32[64,192]{1,0:T(8,128)}, /*index=...) custom-call(s32[6]{0:T(128)S(1)} %stack.33.sc, ...), custom_call_target="tpu_custom_call" | custom-call | flops 1000000 | bytes 9000000 | tf_op jit(solution)/shard_map/final/pallas_call | solution.py:398
  (95 shorter events, 29.7 us)
Async XLA Ops:
  23.2 12.1 %collective-permute-start = (bf16[4,768,768]{2,1,0:T(8,128)(2,1)}, bf16[4,768,768]{2,1,0:T(8,128)(2,1)}, u32[]{:S(2)}, u32[]{:S(2)}) collective-permute-start(bf16[4,768,768]{2,1,0:T(8,128)(2,1)} %get-tuple-element.111), channel_id=1, source_target_pairs={{0,4},{4,0},{8,12},{12,8},{16,20},{20,16},{24,28},{28,24},{1,5},{5... | collective-permute-start | bytes 14155784 | tf_op jit(solution)/shard_map/ppermute | solution.py:465
  35.3 24.8 %collective-permute-start.1 = (bf16[1024,128]{1,0:T(8,128)(2,1)}, bf16[1024,128]{1,0:T(8,128)(2,1)}, u32[]{:S(2)}, u32[]{:S(2)}) collective-permute-start(bf16[1024,128]{1,0:T(8,128)(2,1)} %get-tuple-element.118.kv_ref), channel_id=1, source_target_pairs={{0,1},{2,3},{4,5},{6,7},{8,9},{10,11},{12,13},{14,15},{16,17},{18,... | collective-permute-start | bytes 786440 | tf_op jit(solution)/shard_map/ppermute | solution.py:474
  60.1 29.8 %collective-permute-start.2 = (bf16[4,384,768]{2,1,0:T(8,128)(2,1)}, bf16[4,384,768]{2,1,0:T(8,128)(2,1)S(1)}, u32[]{:S(2)}, u32[]{:S(2)}) collective-permute-start(bf16[4,384,768]{2,1,0:T(8,128)(2,1)} %get-tuple-element.126), channel_id=1, source_target_pairs={{0,8},{4,20},{8,0},{12,28},{16,24},{20,4},{24,16},{28,12},{1,9},{5... | collective-permute-start | bytes 7077896 | tf_op jit(solution)/shard_map/ppermute | solution.py:425
  66.6 23.3 %copy-start.16 = (bf16[4,384,768]{2,1,0:T(8,128)(2,1)S(1)}, bf16[4,384,768]{2,1,0:T(8,128)(2,1)}, u32[]{:S(2)}) copy-start(bf16[4,384,768]{2,1,0:T(8,128)(2,1)} %get-tuple-element.125) | copy-start | bytes 7077892
  89.9 3.5 %copy-start.12 = (bf16[6,1024,128]{2,1,0:T(8,128)(2,1)S(1)}, bf16[6,1024,128]{2,1,0:T(8,128)(2,1)}, u32[]{:S(2)}) copy-start(bf16[6,1024,128]{2,1,0:T(8,128)(2,1)} %get-tuple-element.116.q_ref) | copy-start | bytes 4718596
  89.9 3.5 %copy-start.14 = (bf16[6,1024,128]{2,1,0:T(8,128)(2,1)S(1)}, bf16[6,1024,128]{2,1,0:T(8,128)(2,1)}, u32[]{:S(2)}) copy-start(bf16[6,1024,128]{2,1,0:T(8,128)(2,1)} %get-tuple-element.117.do_ref) | copy-start | bytes 4718596
  90.5 25.9 %collective-permute-start.3 = (bf16[4,192,768]{2,1,0:T(8,128)(2,1)S(1)}, bf16[4,192,768]{2,1,0:T(8,128)(2,1)S(1)}, u32[]{:S(2)}, u32[]{:S(2)}) collective-permute-start(bf16[4,192,768]{2,1,0:T(8,128)(2,1)S(1)} %get-tuple-element.193), channel_id=1, source_target_pairs={{0,16},{4,12},{8,24},{12,4},{16,0},{20,28},{24,8},{28,20},{1,17},{... | collective-permute-start | bytes 3538952 | tf_op jit(solution)/shard_map/ppermute | solution.py:425
  92.1 24.3 %collective-permute-start.4 = (bf16[128,512]{1,0:T(8,128)(2,1)S(1)}, bf16[128,512]{1,0:T(8,128)(2,1)S(1)}, u32[]{:S(2)}, u32[]{:S(2)}) collective-permute-start(bf16[128,512]{1,0:T(8,128)(2,1)S(1)} %get-tuple-element.129), channel_id=1, source_target_pairs={{1,0},{3,2},{5,4},{7,6},{9,8},{11,10},{13,12},{15,14},{17,16},{19,... | collective-permute-start | bytes 393224 | tf_op jit(solution)/shard_map/ppermute | solution.py:484
  116.3 2.7 %copy-start.2 = (bf16[1024,768]{1,0:T(8,128)(2,1)}, bf16[1024,768]{1,0:T(8,128)(2,1)S(1)}, u32[]{:S(2)}) copy-start(bf16[1024,768]{1,0:T(8,128)(2,1)S(1)} %get-tuple-element.134.dq_ref) | copy-start | bytes 4718596
  116.4 2.7 %copy-start.4 = (bf16[1024,768]{1,0:T(8,128)(2,1)}, bf16[1024,768]{1,0:T(8,128)(2,1)S(1)}, u32[]{:S(2)}) copy-start(bf16[1024,768]{1,0:T(8,128)(2,1)S(1)} %get-tuple-element.139.o_ref) | copy-start | bytes 4718596
  116.4 8.4 %collective-permute-start.5 = (bf16[128,512]{1,0:T(8,128)(2,1)S(1)}, bf16[128,512]{1,0:T(8,128)(2,1)S(1)}, u32[]{:S(2)}, u32[]{:S(2)}) collective-permute-start(bf16[128,512]{1,0:T(8,128)(2,1)S(1)} %get-tuple-element.138), channel_id=1, source_target_pairs={{1,0},{3,2},{5,4},{7,6},{9,8},{11,10},{13,12},{15,14},{17,16},{19,... | collective-permute-start | bytes 393224 | tf_op jit(solution)/shard_map/ppermute | solution.py:488
  120.0 4.8 %copy-start.6 = (f32[1024,256]{1,0:T(8,128)S(1)}, f32[1024,256]{1,0:T(8,128)}, u32[]{:S(2)}) copy-start(f32[1024,256]{1,0:T(8,128)} %get-tuple-element.121.tab_ref) | copy-start | bytes 3145732
  128.7 9.7 %collective-permute-start.6 = (bf16[4,96,1664]{2,1,0:T(8,128)(2,1)}, bf16[4,96,1664]{2,1,0:T(8,128)(2,1)}, u32[]{:S(2)}, u32[]{:S(2)}) collective-permute-start(bf16[4,96,1664]{2,1,0:T(8,128)(2,1)} %get-tuple-element.151), channel_id=1, source_target_pairs={{0,4},{4,0},{8,12},{12,8},{16,20},{20,16},{24,28},{28,24},{1,5},{5... | collective-permute-start | bytes 3833864 | tf_op jit(solution)/shard_map/ppermute | solution.py:425
  141.5 17.2 %collective-permute-start.7 = (bf16[4,48,1664]{2,1,0:T(8,128)(2,1)}, bf16[4,48,1664]{2,1,0:T(8,128)(2,1)}, u32[]{:S(2)}, u32[]{:S(2)}) collective-permute-start(bf16[4,48,1664]{2,1,0:T(8,128)(2,1)} %get-tuple-element.195), channel_id=1, source_target_pairs={{0,8},{4,20},{8,0},{12,28},{16,24},{20,4},{24,16},{28,12},{1,9},{5... | collective-permute-start | bytes 1916936 | tf_op jit(solution)/shard_map/ppermute | solution.py:425
  142.2 16.5 %collective-permute-start.8 = (bf16[2,192,768]{2,1,0:T(8,128)(2,1)}, bf16[2,192,768]{2,1,0:T(8,128)(2,1)}, u32[]{:S(2)}, u32[]{:S(2)}) collective-permute-start(bf16[2,192,768]{2,1,0:T(8,128)(2,1)} %get-tuple-element.146), channel_id=1, source_target_pairs={{0,1},{1,0},{2,3},{3,2},{4,5},{5,4},{6,7},{7,6},{8,9},{9,8},{10,11... | collective-permute-start | bytes 1769480 | tf_op jit(solution)/shard_map/ppermute | solution.py:425
  153.1 8.7 %copy-start.15 = (bf16[2,1,192,768]{3,2,1,0:T(8,128)(2,1)S(1)}, bf16[2,1,192,768]{3,2,1,0:T(8,128)(2,1)}, u32[]{:S(2)}) copy-start(bf16[2,1,192,768]{3,2,1,0:T(8,128)(2,1)} %get-tuple-element.196) | copy-start | bytes 1769476
  154.6 21.3 %collective-permute-start.10 = (f32[16,768]{1,0:T(8,128)}, f32[16,768]{1,0:T(8,128)}, u32[]{:S(2)}, u32[]{:S(2)}) collective-permute-start(f32[16,768]{1,0:T(8,128)} %select_maximum_fusion), channel_id=1, source_target_pairs={{0,4},{4,0},{8,12},{12,8},{16,20},{20,16},{24,28},{28,24},{1,5},{5... | collective-permute-start | bytes 147464 | tf_op jit(solution)/shard_map/ppermute | solution.py:519
  160.9 15.0 %collective-permute-start.9 = (bf16[4,24,1664]{2,1,0:T(8,128)(2,1)}, bf16[4,24,1664]{2,1,0:T(8,128)(2,1)}, u32[]{:S(2)}, u32[]{:S(2)}) collective-permute-start(bf16[4,24,1664]{2,1,0:T(8,128)(2,1)} %get-tuple-element.199), channel_id=1, source_target_pairs={{0,16},{4,12},{8,24},{12,4},{16,0},{20,28},{24,8},{28,20},{1,17},{... | collective-permute-start | bytes 958472 | tf_op jit(solution)/shard_map/ppermute | solution.py:425
  163.5 24.8 %collective-permute-start.12 = (bf16[192,768]{1,0:T(8,128)(2,1)}, bf16[192,768]{1,0:T(8,128)(2,1)}, u32[]{:S(2)}, u32[]{:S(2)}) collective-permute-start(bf16[192,768]{1,0:T(8,128)(2,1)} %fusion.7), channel_id=1, source_target_pairs={{0,2},{1,3},{2,0},{3,1},{4,6},{5,7},{6,4},{7,5},{8,10},{9,11},{10,... | collective-permute-start | bytes 884744 | tf_op jit(solution)/shard_map/ppermute | solution.py:425
  179.3 9.0 %collective-permute-start.11 = (bf16[2,24,1664]{2,1,0:T(8,128)(2,1)}, bf16[2,24,1664]{2,1,0:T(8,128)(2,1)}, u32[]{:S(2)}, u32[]{:S(2)}) collective-permute-start(bf16[2,24,1664]{2,1,0:T(8,128)(2,1)} %get-tuple-element.201), channel_id=1, source_target_pairs={{0,1},{1,0},{2,3},{3,2},{4,5},{5,4},{6,7},{7,6},{8,9},{9,8},{10,11... | collective-permute-start | bytes 479240 | tf_op jit(solution)/shard_map/ppermute | solution.py:425
  181.5 6.8 %collective-permute-start.13 = (f32[16,768]{1,0:T(8,128)}, f32[16,768]{1,0:T(8,128)}, u32[]{:S(2)}, u32[]{:S(2)}) collective-permute-start(f32[16,768]{1,0:T(8,128)} %fusion.17), channel_id=1, source_target_pairs={{0,8},{4,20},{8,0},{12,28},{16,24},{20,4},{24,16},{28,12},{1,9},{5... | collective-permute-start | bytes 147464 | tf_op jit(solution)/shard_map/ppermute | solution.py:519
  188.3 10.2 %copy-start.17 = (bf16[2,1,24,1664]{3,2,1,0:T(8,128)(2,1)S(1)}, bf16[2,1,24,1664]{3,2,1,0:T(8,128)(2,1)}, u32[]{:S(2)}) copy-start(bf16[2,1,24,1664]{3,2,1,0:T(8,128)(2,1)} %get-tuple-element.200) | copy-start | bytes 479236
  189.6 7.6 %collective-permute-start.15 = (bf16[192,768]{1,0:T(8,128)(2,1)S(1)}, bf16[192,768]{1,0:T(8,128)(2,1)S(1)}, u32[]{:S(2)}, u32[]{:S(2)}) collective-permute-start(bf16[192,768]{1,0:T(8,128)(2,1)S(1)} %fusion.3), channel_id=1, source_target_pairs={{0,16},{4,12},{8,24},{12,4},{16,0},{20,28},{24,8},{28,20},{1,17},{... | collective-permute-start | bytes 884744 | tf_op jit(solution)/shard_map/ppermute | solution.py:444
  191.1 6.1 %collective-permute-start.14 = (bf16[24,1664]{1,0:T(8,128)(2,1)S(1)}, bf16[24,1664]{1,0:T(8,128)(2,1)S(1)}, u32[]{:S(2)}, u32[]{:S(2)}) collective-permute-start(bf16[24,1664]{1,0:T(8,128)(2,1)S(1)} %fusion.13), channel_id=1, source_target_pairs={{0,2},{1,3},{2,0},{3,1},{4,6},{5,7},{6,4},{7,5},{8,10},{9,11},{10,... | collective-permute-start | bytes 239624 | tf_op jit(solution)/shard_map/ppermute | solution.py:425
  192.3 4.6 %collective-permute-start.16 = (f32[16,768]{1,0:T(8,128)S(1)}, f32[16,768]{1,0:T(8,128)S(1)}, u32[]{:S(2)}, u32[]{:S(2)}) collective-permute-start(f32[16,768]{1,0:T(8,128)S(1)} %add.161), channel_id=1, source_target_pairs={{0,16},{4,12},{8,24},{12,4},{16,0},{20,28},{24,8},{28,20},{1,17},{... | collective-permute-start | bytes 147464 | tf_op jit(solution)/shard_map/ppermute | solution.py:519
  197.2 12.9 %collective-permute-start.20 = (bf16[384,768]{1,0:T(8,128)(2,1)S(1)}, bf16[384,768]{1,0:T(8,128)(2,1)S(1)}, u32[]{:S(2)}, u32[]{:S(2)}) collective-permute-start(bf16[384,768]{1,0:T(8,128)(2,1)S(1)} %pad_maximum_fusion.1), channel_id=1, source_target_pairs={{0,8},{4,20},{8,0},{12,28},{16,24},{20,4},{24,16},{28,12},{1,9},{5... | collective-permute-start | bytes 1769480 | tf_op jit(solution)/shard_map/ppermute | solution.py:444
  199.4 5.4 %collective-permute-start.17 = (bf16[24,1664]{1,0:T(8,128)(2,1)S(1)}, bf16[24,1664]{1,0:T(8,128)(2,1)S(1)}, u32[]{:S(2)}, u32[]{:S(2)}) collective-permute-start(bf16[24,1664]{1,0:T(8,128)(2,1)S(1)} %fusion.10), channel_id=1, source_target_pairs={{0,16},{4,12},{8,24},{12,4},{16,0},{20,28},{24,8},{28,20},{1,17},{... | collective-permute-start | bytes 239624 | tf_op jit(solution)/shard_map/ppermute | solution.py:444
  200.6 4.1 %collective-permute-start.18 = (f32[16,768]{1,0:T(8,128)S(1)}, f32[16,768]{1,0:T(8,128)S(1)}, u32[]{:S(2)}, u32[]{:S(2)}) collective-permute-start(f32[16,768]{1,0:T(8,128)S(1)} %add.164), channel_id=1, source_target_pairs={{0,1},{1,0},{2,3},{3,2},{4,5},{5,4},{6,7},{7,6},{8,9},{9,8},{10,11... | collective-permute-start | bytes 147464 | tf_op jit(solution)/shard_map/ppermute | solution.py:519
  204.8 5.3 %collective-permute-start.19 = (bf16[48,1664]{1,0:T(8,128)(2,1)S(1)}, bf16[48,1664]{1,0:T(8,128)(2,1)S(1)}, u32[]{:S(2)}, u32[]{:S(2)}) collective-permute-start(bf16[48,1664]{1,0:T(8,128)(2,1)S(1)} %pad_maximum_fusion.3), channel_id=1, source_target_pairs={{0,8},{4,20},{8,0},{12,28},{16,24},{20,4},{24,16},{28,12},{1,9},{5... | collective-permute-start | bytes 479240 | tf_op jit(solution)/shard_map/ppermute | solution.py:444
  210.2 5.8 %collective-permute-start.21 = (bf16[768,768]{1,0:T(8,128)(2,1)S(1)}, bf16[768,768]{1,0:T(8,128)(2,1)S(1)}, u32[]{:S(2)}, u32[]{:S(2)}) collective-permute-start(bf16[768,768]{1,0:T(8,128)(2,1)S(1)} %pad_maximum_fusion.m_ref), channel_id=1, source_target_pairs={{0,4},{4,0},{8,12},{12,8},{16,20},{20,16},{24,28},{28,24},{1,5},{5... | collective-permute-start | bytes 3538952 | tf_op jit(solution)/shard_map/ppermute | solution.py:542
  210.3 5.7 %collective-permute-start.22 = (bf16[96,1664]{1,0:T(8,128)(2,1)S(1)}, bf16[96,1664]{1,0:T(8,128)(2,1)S(1)}, u32[]{:S(2)}, u32[]{:S(2)}) collective-permute-start(bf16[96,1664]{1,0:T(8,128)(2,1)S(1)} %pad_maximum_fusion.2.a_ref), channel_id=1, source_target_pairs={{0,4},{4,0},{8,12},{12,8},{16,20},{20,16},{24,28},{28,24},{1,5},{5... | collective-permute-start | bytes 958472 | tf_op jit(solution)/shard_map/ppermute | solution.py:543
  210.9 5.2 %collective-permute-start.23 = (f32[16,768]{1,0:T(8,128)S(1)}, f32[16,768]{1,0:T(8,128)S(1)}, u32[]{:S(2)}, u32[]{:S(2)}) collective-permute-start(f32[16,768]{1,0:T(8,128)S(1)} %add.165.s_ref), channel_id=1, source_target_pairs={{0,2},{1,3},{2,0},{3,1},{4,6},{5,7},{6,4},{7,5},{8,10},{9,11},{10,... | collective-permute-start | bytes 147464 | tf_op jit(solution)/shard_map/ppermute | solution.py:545
  (10 other events, 12.9 us)
where the time goes:
time: 222 us; the launch traced here: 221 us
  Pallas kernels  141 us (64%)
  starting transfers between devices  30.6 us (14%)
  other arithmetic  20.9 us (9%)
  waiting for transfers between devices  18.4 us (8%)
  local copies, waits for them, and re-layouts  9.64 us (4%)
    pallas_call x2, Pallas kernels, attn_row(): pl.pallas_call(body, grid=(NP // 2,), in_specs=ins, out_specs=[ob, ob, c(...  46.2 us
    pallas_call x2, Pallas kernels, mlp_half(): pl.pallas_call(functools.partial(mlp_kernel, last, rows), grid_spec=pltpu...  40 us
    pallas_call x2, Pallas kernels, product(): pl.pallas_call(functools.partial(product_kernel, NT if across else NN), g...  19.4 us
    convert_element_type x9, other arithmetic, add(): return (a.astype(F32) + b.astype(F32)).astype(a.dtype)  14 us
    ppermute x9, starting transfers between devices, go(): self.recv = lax.ppermute(self.send, axis, pairs)  12.6 us
    ppermute x5, waiting for transfers between devices, on_device(): sr = lax.ppermute(small, axis, pairs)  9.68 us
    unnamed x39, local copies, waits for them, and re-layouts  9.48 us
    pallas_call x1, Pallas kernels, pre(): pl.pallas_call(pre_kernel, grid=(N // B,), in_specs=[row(D), row(D), col(...  9.14 us
  transfers between devices with their start and end apart: 24, of which 7 were waited for; matrix products, arithmetic and copies ran while one was open for 7% of the time, Pallas kernels for 51%

commit v1 on v0

--- a/solution.py
+++ b/solution.py
@@ -27,6 +27,8 @@
     return pltpu.CompilerParams(dimension_semantics=("arbitrary",)*n,vmem_limit_bytes=VMEM_ALL if mb is None else mb<<20)
 ANY=pl.BlockSpec(memory_space=pl.ANY)
 hs=jax.ShapeDtypeStruct
+def stay(v):
+    return pltpu.with_memory_space_constraint(v,pltpu.HBM)
 def whole(a):
     z=(0,)*len(a.shape)
     return pl.BlockSpec(a.shape,lambda *_: z)
@@ -184,10 +186,11 @@
         out_shape=outs,input_output_aliases=alias,cost_estimate=cost(4*N*D*F*1.3,20e6),
         compiler_params=params(1,None),name="mlp_keep" if last else "mlp_send")(sc,*args)
 
-def attn_kernel(RB,q_ref,do_ref,kv_ref,kvp_ref,tab_ref,o_ref,dq_ref,dk_ref,dp_out,kx_ref,bias_ref,s_ref,d_ref,p_ref,ds_ref,acc_ref,qt_ref,oa_ref):
-    step=pl.program_id(0)
+def attn_kernel(base,per,RB,acc_in,q_ref,do_ref,kv_ref,kvp_ref,tab_ref,o_ref,dq_ref,own_ref,prev_ref,rest_ref,kx_ref,bias_ref,s_ref,d_ref,p_ref,ds_ref,acc_ref,qt_ref,oa_ref):
+    first=pl.program_id(0)==0
+    step=lax.rem(pl.program_id(0)+base,per)
     T=q_ref.shape[1]; QB=T//2
-    @pl.when(step==0)
+    @pl.when(first|(step==0))
     def _():
         for i,ref in enumerate((kvp_ref,kv_ref)):
             kv=ref[...].astype(F32)
@@ -206,7 +209,8 @@
             bias_ref[r,:]=jnp.where(ok,0.0,NEG)
             return 0
         lax.fori_loop(0,T//64,mask,0)
-        acc_ref[...]=jnp.zeros_like(acc_ref)
+        if acc_in is None: acc_ref[...]=jnp.zeros_like(acc_ref)
+        else: acc_ref[...]=acc_in[...]
     def run(lo):
         units=[(qb,e) for qb in (0,1) for e in (0,1)]
         rng=lambda qb: (lo,T+(qb+1)*QB)
@@ -251,28 +255,39 @@
         mm2(2); vp(3)
         mm2(3)
     run(0)
-    @pl.when(step==pl.num_programs(0)-1)
+    @pl.when(step==per-1)
     def _():
-        dp_out[...]=acc_ref[:,:T].astype(BF)
-        dk_ref[...]=acc_ref[:,T:]
-def attn_row(row,q,do,kv,kvp,tab,prev=None,T=512,RB=32):
-    NP,N,_=q.shape; QB=T//2
+        prev_ref[...]=acc_ref[:,:T].astype(BF)
+        own_ref[...]=acc_ref[:,T:]
+    if rest_ref is not None:
+        @pl.when(pl.program_id(0)==pl.num_programs(0)-1)
+        def _(): rest_ref[...]=acc_ref[...]
+def attn_part(base,count,q,do,kv,kvp,tab,prev=None,T=512,RB=32):
+    NP,N,_=q.shape; QB=T//2; per=NP//2
     bf=BF; f=F32
-    hb=pl.BlockSpec((2,T,128),lambda h:(h,row,0)); rb=lambda w: pl.BlockSpec((T,w),lambda h:(row,0))
-    def body(q_ref,do_ref,kv_ref,kvp_ref,tab_ref,*rest):
-        if prev is not None: rest=rest[2:]
-        attn_kernel(RB,q_ref,do_ref,kv_ref,kvp_ref,tab_ref,*rest)
-    ins=[hb,hb,rb(128),rb(128),rb(256)]; args=[q,do,kv,kvp,tab]; alias={}
-    if prev is not None:
-        ins+=[ANY,ANY]; args+=list(prev); alias={5:0,6:1}
-    c=lambda: pl.BlockSpec((128,T),lambda h:(0,0)); ob=pl.BlockSpec((T,256),lambda h:(row,h))
+    row=lambda h: lax.div(h+base,per); col=lambda h: lax.rem(h+base,per)
+    hb=pl.BlockSpec((2,T,128),lambda h:(col(h),row(h),0)); rb=lambda w: pl.BlockSpec((T,w),lambda h:(row(h),0))
+    c=lambda w: pl.BlockSpec((128,w),lambda h:(0,0)); ob=pl.BlockSpec((T,256),lambda h:(row(h),col(h)))
+    more=prev is not None
+    def body(q_ref,do_ref,kv_ref,kvp_ref,tab_ref,*refs):
+        acc_in=None
+        if more: acc_in=refs[0]; refs=refs[3:]
+        o_ref,dq_ref,own_ref,prev_ref,*refs=refs
+        rest_ref=None
+        if not more: rest_ref,*refs=refs
+        attn_kernel(base,per,RB,acc_in,q_ref,do_ref,kv_ref,kvp_ref,tab_ref,o_ref,dq_ref,own_ref,prev_ref,rest_ref,*refs)
+    ins=[hb,hb,rb(128),rb(128),rb(256)]; args=[stay(v) for v in (q,do,kv,kvp,tab)]; alias={}
+    outs=[hs((N,NP*128),bf)]*2+[hs((128,T),f),hs((128,T),bf)]; specs=[ob,ob,c(T),c(T)]
+    if more:
+        ins+=[c(2*T),ANY,ANY]; args+=[prev[2],prev[0],prev[1]]; alias={6:0,7:1}
+    else:
+        outs+=[hs((128,2*T),f)]; specs+=[c(2*T)]
     return pl.pallas_call(body,
-      grid=(NP//2,),in_specs=ins,out_specs=[ob,ob,c(),c()],
+      grid=(count,),in_specs=ins,out_specs=specs,
         scratch_shapes=[pltpu.VMEM((4,2*T,128),bf),pltpu.VMEM((T,2*T),f),pltpu.VMEM((2,2*QB,2*T),f),pltpu.VMEM((2,2*QB,2*T),f),
                         pltpu.VMEM((2,2*QB,2*T),bf),pltpu.VMEM((2,2*QB,2*T),bf),pltpu.VMEM((128,2*T),f),pltpu.VMEM((2,2,128,2*QB),bf),pltpu.VMEM((2,2*QB,128),f)],
-      out_shape=[hs((N,NP*128),bf)]*2+[hs((128,T),f),hs((128,T),bf)],
-      input_output_aliases=alias,cost_estimate=cost(2.4e10,4e6),
-      compiler_params=params(1,28),name=f"attn{row}")(*args)
+      out_shape=outs,input_output_aliases=alias,cost_estimate=cost(8e9*count,1.4e6*count),
+      compiler_params=params(1,28),name="attn_b" if more else "attn_a")(*args)
 def wgrad_kernel(sc,g_ref,o_ref,dq_ref,ai_ref,keep_ref,send_ref,qb_ref,ot_ref,so_ref,sa_ref):
     N,D=o_ref.shape; hr=D//8
     def turn(i,_):
@@ -331,10 +346,12 @@
     return pl.pallas_call(functools.partial(product_kernel,NT if across else NN),grid=(F//D,),
       in_specs=[pl.BlockSpec((N,D),lambda j:(0,j)),ws],out_specs=pl.BlockSpec((N,D),lambda j:(0,0)),out_shape=hs((N,D),F32),
       cost_estimate=cost(4.8e9,1.4e7),compiler_params=params(1,None),name=name)(a,w)
-def postb_kernel(x_ref,g_ref,dq_ref,dkv_ref,c2_ref,wq_ref,wk_ref,wv_ref,vec_ref,ig_ref,sm_ref):
+def postb_kernel(x_ref,g_ref,dq_ref,dkv_ref,c2_ref,wq_ref,wk_ref,wv_ref,vec_ref,qb_ref,hb_ref,kvb_ref,ig_ref,sm_ref):
     j=pl.program_id(0)
     @pl.when(j==0)
-    def _(): sm_ref[...]=jnp.zeros_like(sm_ref)
+    def _():
+        sm_ref[...]=jnp.zeros_like(sm_ref)
+        sm_ref[5:6,:]=qb_ref[...]; sm_ref[6:10,:]=hb_ref[...]; sm_ref[10:11,:kvb_ref.shape[1]]=kvb_ref[...]
     g=g_ref[...].astype(F32)
     n,s=ln(x_ref[...].astype(F32))
     dkv=dkv_ref[...]
@@ -344,13 +361,13 @@
     ig_ref[...]=g+s*(u-jnp.mean(u,-1,keepdims=True)-n*jnp.mean(u*n,-1,keepdims=True))
     for i,v in enumerate((c1*n,c1,c2*n,c2,g)):
         sm_ref[i:i+1,:]+=jnp.sum(v,0,keepdims=True)
-def postb(x,g,dq,dkv,c2,wq,wk,wv,vec,B=256):
+def postb(x,g,dq,dkv,c2,wq,wk,wv,vec,qb,hb,kvb,B=256):
     N,D=x.shape
     return pl.pallas_call(postb_kernel,grid=(N//B,),
-      in_specs=[rows_of(D,B)]*3+[rows_of(128,B),rows_of(D,B)]+[whole(a) for a in (wq,wk,wv,vec)],
-      out_specs=[rows_of(D,B),pl.BlockSpec((8,D),lambda j:(0,0))],
-      out_shape=[hs((N,D),F32),hs((8,D),F32)],
-      cost_estimate=cost(2e9,1.2e7),compiler_params=params(1,None),name="postb")(x,g,dq,dkv,c2,wq,wk,wv,vec)
+      in_specs=[rows_of(D,B)]*3+[rows_of(128,B),rows_of(D,B)]+[whole(a) for a in (wq,wk,wv,vec,qb,hb,kvb)],
+      out_specs=[rows_of(D,B),pl.BlockSpec((16,D),lambda j:(0,0))],
+      out_shape=[hs((N,D),F32),hs((16,D),F32)],
+      cost_estimate=cost(2e9,1.2e7),compiler_params=params(1,None),name="postb")(x,g,dq,dkv,c2,wq,wk,wv,vec,qb,hb,kvb)
 def posta_kernel(x_ref,o_ref,mb_ref,wo_ref,vec_ref,lo_ref):
     lo_ref[...]=(x_ref[...].astype(F32)+(dotf(o_ref[...],wo_ref[...])+vec_ref[V_O:V_O+1,:])+(mb_ref[...]+vec_ref[V_D:V_D+1,:])).astype(BF)
 def posta(x,o,mb,wo,vec,B=256):
@@ -360,7 +377,7 @@
       out_specs=rows_of(D,B),out_shape=hs((N,D),BF),
       cost_estimate=cost(2e9,9e6),compiler_params=params(1,None),name="posta")(x,o,mb,wo,vec)
 def final_kernel(sc,m_ref,mr_ref,a_ref,ar_ref,s_ref,sr_ref,w1_ref,w2_ref,wo_ref,wq_ref,wk_ref,wv_ref,
-                 n1g_ref,n1b_ref,n2g_ref,n2b_ref,ob_ref,qb_ref,hb_ref,kb_ref,vb_ref,kv_ref):
+                 n1g_ref,n1b_ref,n2g_ref,n2b_ref,ob_ref,qb_ref,db_ref,hb_ref,kb_ref,vb_ref,kv_ref):
     W=w2_ref.shape[0]//2; D=m_ref.shape[1]; q=D//4; hr=a_ref.shape[0]; pr=hr//4; mr=m_ref.shape[0]//4
     for r0,(m,a) in enumerate(((m_ref,a_ref),(mr_ref,ar_ref))):
         h=sc[0]^r0
@@ -389,12 +406,13 @@
         def _():
             for k,ref in enumerate((n1g_ref,n1b_ref,n2g_ref,n2b_ref,ob_ref,qb_ref)):
                 ref[...]=t[k:k+1,s*q:(s+1)*q].reshape(q)
+            db_ref[...]=t[4:5,s*q:(s+1)*q].reshape(q)
             hb_ref[...]=t[6+s:7+s,:].reshape(D)
             n=kb_ref.shape[0]; kb_ref[...]=t[10:11,s*n:(s+1)*n].reshape(n)
             n=vb_ref.shape[0]; vb_ref[...]=t[10:11,64+s*n:64+(s+1)*n].reshape(n)
 def final(sc,m,mr,a,ar,s,sr,F,rotd):
     D=m.shape[1]; f=F32; v=hs((D//4,),f)
-    outs=[hs((D//4,F),f),hs((F//4,D),f),hs((D//4,D),f),hs((D//4,D),f),hs((64,D//4),f),hs((64,D//4),f)]+[v]*6+[hs((D,),f),hs((rotd//4,),f),hs((16,),f)]
+    outs=[hs((D//4,F),f),hs((F//4,D),f),hs((D//4,D),f),hs((D//4,D),f),hs((64,D//4),f),hs((64,D//4),f)]+[v]*7+[hs((D,),f),hs((rotd//4,),f),hs((16,),f)]
     return pl.pallas_call(final_kernel,
         grid_spec=pltpu.PrefetchScalarGridSpec(num_scalar_prefetch=1,grid=(1,),in_specs=[whole(u) for u in (m,mr,a,ar,s,sr)],out_specs=[whole(u) for u in outs],
             scratch_shapes=[pltpu.VMEM((D//4,128),F32)]),
@@ -460,7 +478,7 @@
     vec=table(norm1_gain,norm1_bias,norm2_gain,norm2_bias,query_bias,output_bias,down_bias,key_bias,value_bias,hidden_bias)
     pos=lax.dynamic_slice_in_dim(positions,s*T,T,1)
     st=dp_stages(); core=st[0][0]; bit1=st[1][0]
-    back=[(i+1,i) for i in range(0,sp,2)]
+    both=[(i,i^1) for i in range(sp)]
     Ms,act,gp,dbs,mi=mlp_half(jnp.stack([1-core,bit1]),x,g,hidden_weight,down_weight,vec)
     Mr=lax.ppermute(Ms,"dp",st[0][1])
     pf=pos.astype(F32).reshape(N)
@@ -471,21 +489,21 @@
     xq,=after([x],dbs)
     q,kv,do,tab,ai=pre(xq,g,cs,query_weight,key_weight.T,value_weight.T,output_weight,vec)
     kv,Mr=after([kv,Mr],q)
-    kvp=lax.ppermute(kv,"sp",[(i,i+1) for i in range(0,sp,2)])
+    kvp=lax.ppermute(kv,"sp",both)
     mi,=after([mi],q)
     keep,send,act,gp,dbk=mlp_half(jnp.stack([core,bit1]),mi,g,hidden_weight,down_weight,vec,recv=Mr,dbs=dbs,act=act,gp=gp)
     M=Stream(st,1,send,keep)
     M.send,kvp=after([M.send,kvp],dbk)
     M.go()
     q,=after([q],dbk)
-    o,dq,d0,k0=attn_row(0,q,do,kv,kvp,tab,T=T)
+    o,dq,d0,k0,part=attn_part(0,2*(D//256)*2//3,q,do,kv,kvp,tab,T=T)
     M.recv,k0=after([M.recv,k0],dq)
     M.land()
-    r0=lax.ppermute(k0,"sp",back); M.go()
+    r0=lax.ppermute(k0,"sp",both); M.go()
     o,dq=after([o,dq],M.send,k0)
-    o,dq,d1,k1=attn_row(1,q,do,kv,kvp,tab,prev=(o,dq),T=T)
+    o,dq,d1,k1=attn_part(2*(D//256)*2//3,2*(D//256)-2*(D//256)*2//3,q,do,kv,kvp,tab,prev=(o,dq,part),T=T)
     k1,M.recv,r0=after([k1,M.recv,r0],dq)
-    r1=lax.ppermute(k1,"sp",back)
+    r1=lax.ppermute(k1,"sp",both)
     while True:
         M.land()
         if M.at>=len(st): break
@@ -521,7 +539,7 @@
         if fill:
             k=fill.pop(0)
             if k=="c2": gk,=after([gp],*moved); c2=product(gk,hidden_weight,True,"back"); deps=[c2]
-            if k=="ig": xk,=after([x],*moved); ig,sm=postb(xk,g,dq,dkv,c2,query_weight,key_weight.T,value_weight.T,vec); deps=[ig]
+            if k=="ig": xk,=after([x],*moved); ig,sm=postb(xk,g,dq,dkv,c2,query_weight,key_weight.T,value_weight.T,vec,qb,dbk,kvb); deps=[ig]
             if k=="mb": ak,=after([act],*moved); mb=product(ak,down_weight,False,"down"); deps=[mb]
             if k=="lo": xk,=after([x],*moved); lo=posta(xk,o,mb,output_weight,vec); deps=[lo]
         lands=busy and held==0
@@ -538,15 +556,15 @@
             else: M.gather_land()
         held-=1
         if small is None and ig is not None:
-            small=jnp.concatenate([sm[:5],qb,dbk,jnp.pad(kvb,((0,5),(0,D-kvb.shape[1])))],0)
+            small=sm
     Mr=lax.ppermute(M.own,"dp",st[0][1])
     Ar=lax.ppermute(A.own,"dp",st[0][1])
     axis,pairs=todo.pop(0)
     sr=lax.ppermute(small,axis,pairs)
     zero=jnp.zeros_like(core)
     where=jnp.stack([core,s]+[st[t][of] if len(st)>t else zero for of in (0,2) for t in (1,2)])
-    rw1,rw2,ro,rq,rk,rv,n1g,n1b,n2g,n2b,ob,qbg,hb,kb,vb=final(where,M.settle(M.own,0),M.settle(Mr,2),A.settle(A.own,0),A.settle(Ar,2),small,sr,F,rotd)
-    return (lo.reshape(R,T,D),ig.reshape(R,T,D),n1g,n1b,n2g,n2b,rq,qbg,rk.T,kb,rv.T,vb,ro,ob,rw1,hb,rw2,ob)
+    rw1,rw2,ro,rq,rk,rv,n1g,n1b,n2g,n2b,ob,qbg,db,hb,kb,vb=final(where,M.settle(M.own,0),M.settle(Mr,2),A.settle(A.own,0),A.settle(Ar,2),small,sr,F,rotd)
+    return (lo.reshape(R,T,D),ig.reshape(R,T,D),n1g,n1b,n2g,n2b,rq,qbg,rk.T,kb,rv.T,vb,ro,ob,rw1,hb,rw2,db)
 def solution(mesh):
     t=P("dp","sp",None); m=P("dp",None); w=P()
     v=P("sp"); v2=P("sp",None)

time: 222 us -> 214 us (0.964)
  local copies, waits for them, and re-layouts: 9.64 us -> 3.49 us
  starting transfers between devices: 30.6 us -> 24.6 us
  waiting for transfers between devices: 18.4 us -> 21.9 us
    unnamed x39 -> x26, local copies, waits for them, and re-layouts: 9.48 us -> 3.33 us
    ppermute x3, starting transfers between devices: 7.78 us -> 4.74 us  [the longest x1 2.66 us: on_device(): kvp = lax.ppermute(kv, 'sp', both)]
    ppermute x9, starting transfers between devices: 12.6 us -> 9.75 us  [go(): self.recv = lax.ppermute(self.send, axis, pairs)]
    ppermute x9, waiting for transfers between devices: 4.34 us -> 6.88 us  [go(): self.recv = lax.ppermute(self.send, axis, pairs)]
  transfers between devices with their start and end apart: 24 -> 24, of which waited for: 7 -> 7; matrix products, arithmetic and copies ran while one was open for 7% -> 7% of each run, Pallas kernels for 51% -> 54%
where the time goes in v1:
time: 214 us; the launch traced here: 213 us
  Pallas kernels  142 us (66%)
  starting transfers between devices  24.6 us (11%)
  waiting for transfers between devices  21.9 us (10%)
  other arithmetic  19.3 us (9%)
  local copies, waits for them, and re-layouts  3.49 us (2%)
    pallas_call x2, Pallas kernels, attn_part(): pl.pallas_call(body, grid=(count,), in_specs=ins, out_specs=specs, scratc...  47.8 us
    pallas_call x2, Pallas kernels, mlp_half(): pl.pallas_call(functools.partial(mlp_kernel, last, rows), grid_spec=pltpu...  40 us
    pallas_call x2, Pallas kernels, product(): pl.pallas_call(functools.partial(product_kernel, NT if across else NN), g...  19.4 us
    convert_element_type x9, other arithmetic, add(): return (a.astype(F32) + b.astype(F32)).astype(a.dtype)  14 us
    ppermute x5, waiting for transfers between devices, on_device(): sr = lax.ppermute(small, axis, pairs)  10.3 us
    ppermute x9, starting transfers between devices, go(): self.recv = lax.ppermute(self.send, axis, pairs)  9.75 us
    pallas_call x1, Pallas kernels, pre(): pl.pallas_call(pre_kernel, grid=(N // B,), in_specs=[row(D), row(D), col(...  9.13 us
    pallas_call x1, Pallas kernels, postb(): pl.pallas_call(postb_kernel, grid=(N // B,), in_specs=[rows_of(D, B)] * 3...  8.27 us
  transfers between devices with their start and end apart: 24, of which 7 were waited for; matrix products, arithmetic and copies ran while one was open for 7% of the time, Pallas kernels for 54%

profile of v1, /device:TPU:0, one launch (start us, length us, event | category | flops | bytes accessed | tf_op | source)
XLA Modules:
  0.0 212.7 jit_solution(6027794433815302394)
XLA Ops:
  1.3 1.5 table.1.refs_7_.vec_ref
  2.8 20.4 %mlp_send.1 = (bf16[4,768,768]{2,1,0:T(8,128)(2,1)}, bf16[1024,3072]{1,0:T(8,128)(2,1)}, bf16[1024,3072]{1,0:T(8,128)(2,1)}, f32[2,1,768]{2,1,0:T(1,128)}, bf16[1024,768]{1,0:T(8,128)(2,1)}) custom-call(s32[2]{0:T(128)} %get-tuple-element.208.refs_0_, bf16[1024,768]{1,0:T(8,128)(2,1)} %bitcast.88, bf16[1024,768]{1,0:T(8,128)(2,1)} %bitcast.83, ...), custom_call_target="tpu_custom_call" | custom-call | flops 12562779136 | bytes 20000000 | tf_op jit(solution)/shard_map/mlp_send/pallas_call | solution.py:182
  26.2 9.1 %pre.1 = (bf16[6,1024,128]{2,1,0:T(8,128)(2,1)}, bf16[1024,128]{1,0:T(8,128)(2,1)}, bf16[6,1024,128]{2,1,0:T(8,128)(2,1)}, f32[1024,256]{1,0:T(8,128)}, bf16[768,1024]{1,0:T(8,128)(2,1)}) custom-call(bf16[1024,768]{1,0:T(8,128)(2,1)} %bitcast.89, bf16[1024,768]{1,0:T(8,128)(2,1)} %bitcast.84, f32[24,1024]{1,0:T(8,128)} %maximum_maximum_fusion.cs_ref, ...), custom_call_target="tpu_custom_call" | custom-call | flops 4000000000 | bytes 10000000 | tf_op jit(solution)/shard_map/pre/pallas_call | solution.py:87
  35.3 2.7 %collective-permute-start.1 = (bf16[1024,128]{1,0:T(8,128)(2,1)}, bf16[1024,128]{1,0:T(8,128)(2,1)}, u32[]{:S(2)}, u32[]{:S(2)}) collective-permute-start(bf16[1024,128]{1,0:T(8,128)(2,1)} %get-tuple-element.120.kv_ref), channel_id=1, source_target_pairs={{0,1},{1,0},{2,3},{3,2},{4,5},{5,4},{6,7},{7,6},{8,9},{9,8},{10,11... | collective-permute-start | bytes 786440 | tf_op jit(solution)/shard_map/ppermute | solution.py:492
  38.0 19.6 %mlp_keep.1 = (bf16[4,384,768]{2,1,0:T(8,128)(2,1)}, bf16[4,384,768]{2,1,0:T(8,128)(2,1)}, bf16[1024,3072]{1,0:T(8,128)(2,1)}, bf16[1024,3072]{1,0:T(8,128)(2,1)}, f32[4,768]{1,0:T(4,128)}) custom-call(s32[2]{0:T(128)} %get-tuple-element.209.refs_0_, bf16[1024,768]{1,0:T(8,128)(2,1)} %get-tuple-element.111.refs_1_, ...), custom_call_target="tpu_custom_call", output_to_operand_aliasing={{2}: (11, {}), {3}: (12, {})} | custom-call | flops 12562779136 | bytes 20000000 | tf_op jit(solution)/shard_map/mlp_keep/pallas_call | solution.py:182
  57.6 1.6 collective-permute-start.2
  59.1 31.5 %attn_a.1 = (bf16[1024,768]{1,0:T(8,128)(2,1)S(1)}, bf16[1024,768]{1,0:T(8,128)(2,1)S(1)}, f32[128,512]{1,0:T(8,128)S(1)}, bf16[128,512]{1,0:T(8,128)(2,1)S(1)}, f32[128,1024]{1,0:T(8,128)S(1)}) custom-call(bf16[6,1024,128]{2,1,0:T(8,128)(2,1)} %get-tuple-element.118.q_ref, bf16[6,1024,128]{2,1,0:T(8,128)(2,1)} %get-tuple-element.119.do_ref, ...), custom_call_target="tpu_custom_call" | custom-call | flops 32000000000 | bytes 5600000 | tf_op jit(solution)/shard_map/attn_a/pallas_call | solution.py:285
  91.2 1.6 collective-permute-start.3
  93.2 16.3 %attn_b.1 = (bf16[1024,768]{1,0:T(8,128)(2,1)S(1)}, bf16[1024,768]{1,0:T(8,128)(2,1)S(1)}, f32[128,512]{1,0:T(8,128)S(1)}, bf16[128,512]{1,0:T(8,128)(2,1)S(1)}) custom-call(bf16[6,1024,128]{2,1,0:T(8,128)(2,1)} %get-tuple-element.118.q_ref, bf16[6,1024,128]{2,1,0:T(8,128)(2,1)} %get-tuple-element.119.do_ref, ...), custom_call_target="tpu_custom_call", output_to_operand_aliasing={{0}: (6, {}), {1}: (7, {})} | custom-call | flops 16000000000 | bytes 2800000 | tf_op jit(solution)/shard_map/attn_b/pallas_call | solution.py:285
  109.5 1.6 collective-permute-start.5
  113.5 4.8 %wgrad.1 = (bf16[4,96,1664]{2,1,0:T(8,128)(2,1)S(1)}, bf16[4,96,1664]{2,1,0:T(8,128)(2,1)}, f32[1,768]{1,0:T(1,128)S(1)}) custom-call(s32[1]{0:T(128)} %bitcast.1.sc, bf16[1024,768]{1,0:T(8,128)(2,1)S(1)} %bitcast.87, bf16[1024,768]{1,0:T(8,128)(2,1)S(1)} %get-tuple-element.142.o_ref, bf16[1024,768]{1,0:T(8,128)(2,1)S(1)} %get-tuple-element.137.dq_ref, ...), custom_call_target="tpu_custom_call" | custom-call | flops 2600000000 | bytes 9000000 | tf_op jit(solution)/shard_map/wgrad/pallas_call | solution.py:315
  118.3 1.7 kvgrad.1
  122.2 9.7 %back.1.c2_ref = f32[1024,768]{1,0:T(8,128)} custom-call(bf16[1024,3072]{1,0:T(8,128)(2,1)} %get-tuple-element.156.a_ref, bf16[768,3072]{1,0:T(8,128)(2,1)} %w_ref.2), custom_call_target="tpu_custom_call" | custom-call | flops 4800000000 | bytes 14000000 | tf_op jit(solution)/shard_map/back/pallas_call | solution.py:346
  132.0 3.0 %add_convert_fusion.3 = (bf16[4,1,48,1664]{3,2,0,1:T(8,128)(2,1)}, bf16[4,48,1664]{2,1,0:T(8,128)(2,1)}) fusion(bf16[4,2,48,1664]{3,2,1,0:T(8,128)(2,1)} %bitcast.14, s32[]{:T(128)S(6)} %select_n.69, bf16[4,2,48,1664]{3,2,1,0:T(8,128)(2,1)} %bitcast.82, s32[]{:T(128)S(6)} %select_n.70), kind=kLoop, calls=%fused_computation.3 | loop fusion | flops 2555904 | bytes 3833864 | tf_op jit(solution)/shard_map/convert_element_type | solution.py:435
  136.5 8.3 %postb.1 = (f32[1024,768]{1,0:T(8,128)}, f32[16,768]{1,0:T(8,128)}) custom-call(bf16[1024,768]{1,0:T(8,128)(2,1)} %bitcast.90, bf16[1024,768]{1,0:T(8,128)(2,1)} %bitcast.86, bf16[1024,768]{1,0:T(8,128)(2,1)} %copy-done.2, bf16[1024,128]{1,0:T(8,128)(2,1)} %copy-done.6, f32[1024,768]{1,0:T(8,128)} %back.1.c2_ref, bf16[768,768]{1,0:T(8,128)(2,1)} %wq_ref.3, ...), custom_call_target="tpu_custom_call" | custom-call | flops 2000000000 | bytes 12000000 | tf_op jit(solution)/shard_map/postb/pallas_call | solution.py:366
  144.9 6.4 %collective-permute-done.8 = bf16[2,192,768]{2,1,0:T(8,128)(2,1)} collective-permute-done((bf16[2,192,768]{2,1,0:T(8,128)(2,1)}, bf16[2,192,768]{2,1,0:T(8,128)(2,1)}, u32[]{:S(2)}, u32[]{:S(2)}) %collective-permute-start.8) | collective-permute-done | bytes 589856 | tf_op jit(solution)/shard_map/ppermute | solution.py:443
  151.3 2.2 %add_convert_fusion.7 = (bf16[4,1,24,1664]{3,2,1,0:T(8,128)(2,1)}, bf16[4,24,1664]{2,1,0:T(8,128)(2,1)}) fusion(bf16[4,2,24,1664]{3,2,1,0:T(8,128)(2,1)} %bitcast.17, s32[]{:T(128)S(6)} %select_n.67, bf16[4,2,24,1664]{3,2,1,0:T(8,128)(2,1)} %bitcast.93, s32[]{:T(128)S(6)} %select_n.66), kind=kLoop, calls=%fused_computation.10 | loop fusion | flops 1277952 | bytes 1916936 | tf_op jit(solution)/shard_map/convert_element_type | solution.py:435
  154.6 1.7 fusion.7
  156.3 2.6 %collective-permute-start.12 = (bf16[192,768]{1,0:T(8,128)(2,1)}, bf16[192,768]{1,0:T(8,128)(2,1)}, u32[]{:S(2)}, u32[]{:S(2)}) collective-permute-start(bf16[192,768]{1,0:T(8,128)(2,1)} %fusion.7), channel_id=1, source_target_pairs={{0,2},{1,3},{2,0},{3,1},{4,6},{5,7},{6,4},{7,5},{8,10},{9,11},{10,... | collective-permute-start | bytes 884744 | tf_op jit(solution)/shard_map/ppermute | solution.py:443
  158.9 9.7 %down.1.mb_ref = f32[1024,768]{1,0:T(8,128)} custom-call(bf16[1024,3072]{1,0:T(8,128)(2,1)} %get-tuple-element.166.a_ref, bf16[3072,768]{1,0:T(8,128)(2,1)} %w_ref.3), custom_call_target="tpu_custom_call" | custom-call | flops 4800000000 | bytes 14000000 | tf_op jit(solution)/shard_map/down/pallas_call | solution.py:346
  168.6 2.0 add_convert_fusion.8
  170.6 1.4 add.153
  174.0 5.9 %posta.1 = bf16[1024,768]{1,0:T(8,128)(2,1)} custom-call(bf16[1024,768]{1,0:T(8,128)(2,1)} %bitcast.91, bf16[1024,768]{1,0:T(8,128)(2,1)} %copy-done.4, f32[1024,768]{1,0:T(8,128)} %down.1.mb_ref, bf16[768,768]{1,0:T(8,128)(2,1)} %wo_ref.3, f32[12,768]{1,0:T(8,128)} %table.1.refs_7_.vec_ref), custom_call_target="tpu_custom_call" | custom-call | flops 2000000000 | bytes 9000000 | tf_op jit(solution)/shard_map/posta/pallas_call | solution.py:375
  179.9 1.3 fusion.3
  184.0 1.5 collective-permute-start.16
  185.5 3.1 %collective-permute-done.16 = f32[16,768]{1,0:T(8,128)S(1)} collective-permute-done((f32[16,768]{1,0:T(8,128)S(1)}, f32[16,768]{1,0:T(8,128)S(1)}, u32[]{:S(2)}, u32[]{:S(2)}) %collective-permute-start.16) | collective-permute-done | bytes 49184 | tf_op jit(solution)/shard_map/ppermute | solution.py:537
  189.0 1.6 collective-permute-start.20
  192.9 3.8 %collective-permute-done.18 = f32[16,768]{1,0:T(8,128)S(1)} collective-permute-done((f32[16,768]{1,0:T(8,128)S(1)}, f32[16,768]{1,0:T(8,128)S(1)}, u32[]{:S(2)}, u32[]{:S(2)}) %collective-permute-start.18) | collective-permute-done | bytes 49184 | tf_op jit(solution)/shard_map/ppermute | solution.py:537
  197.8 4.5 %collective-permute-done.19 = bf16[48,1664]{1,0:T(8,128)(2,1)S(1)} collective-permute-done((bf16[48,1664]{1,0:T(8,128)(2,1)S(1)}, bf16[48,1664]{1,0:T(8,128)(2,1)S(1)}, u32[]{:S(2)}, u32[]{:S(2)}) %collective-permute-start.19) | collective-permute-done | bytes 159776 | tf_op jit(solution)/shard_map/ppermute | solution.py:462
  203.0 2.0 collective-permute-start.23
  205.2 3.4 %collective-permute-done.23.sr_ref = f32[16,768]{1,0:T(8,128)S(1)} collective-permute-done((f32[16,768]{1,0:T(8,128)S(1)}, f32[16,768]{1,0:T(8,128)S(1)}, u32[]{:S(2)}, u32[]{:S(2)}) %collective-permute-start.23) | collective-permute-done | bytes 49184 | tf_op jit(solution)/shard_map/ppermute | solution.py:563
  208.6 3.9 %final.1 = (f32[192,3072]{1,0:T(8,128)}, f32[768,768]{1,0:T(8,128)}, f32[192,768]{1,0:T(8,128)}, f32[192,768]{1,0:T(8,128)}, f32[64,192]{1,0:T(8,128)}, /*index=...) custom-call(s32[6]{0:T(128)S(1)} %stack.33.sc, ...), custom_call_target="tpu_custom_call" | custom-call | flops 1000000 | bytes 9000000 | tf_op jit(solution)/shard_map/final/pallas_call | solution.py:416
  (81 shorter events, 21.4 us)
Async XLA Ops:
  23.2 12.1 %collective-permute-start = (bf16[4,768,768]{2,1,0:T(8,128)(2,1)}, bf16[4,768,768]{2,1,0:T(8,128)(2,1)}, u32[]{:S(2)}, u32[]{:S(2)}) collective-permute-start(bf16[4,768,768]{2,1,0:T(8,128)(2,1)} %get-tuple-element.113), channel_id=1, source_target_pairs={{0,4},{4,0},{8,12},{12,8},{16,20},{20,16},{24,28},{28,24},{1,5},{5... | collective-permute-start | bytes 14155784 | tf_op jit(solution)/shard_map/ppermute | solution.py:483
  35.3 22.2 %collective-permute-start.1 = (bf16[1024,128]{1,0:T(8,128)(2,1)}, bf16[1024,128]{1,0:T(8,128)(2,1)}, u32[]{:S(2)}, u32[]{:S(2)}) collective-permute-start(bf16[1024,128]{1,0:T(8,128)(2,1)} %get-tuple-element.120.kv_ref), channel_id=1, source_target_pairs={{0,1},{1,0},{2,3},{3,2},{4,5},{5,4},{6,7},{7,6},{8,9},{9,8},{10,11... | collective-permute-start | bytes 786440 | tf_op jit(solution)/shard_map/ppermute | solution.py:492
  57.6 33.0 %collective-permute-start.2 = (bf16[4,384,768]{2,1,0:T(8,128)(2,1)}, bf16[4,384,768]{2,1,0:T(8,128)(2,1)S(1)}, u32[]{:S(2)}, u32[]{:S(2)}) collective-permute-start(bf16[4,384,768]{2,1,0:T(8,128)(2,1)} %get-tuple-element.129), channel_id=1, source_target_pairs={{0,8},{4,20},{8,0},{12,28},{16,24},{20,4},{24,16},{28,12},{1,9},{5... | collective-permute-start | bytes 7077896 | tf_op jit(solution)/shard_map/ppermute | solution.py:443
  59.1 31.5 %copy-start.10 = (bf16[4,384,768]{2,1,0:T(8,128)(2,1)S(1)}, bf16[4,384,768]{2,1,0:T(8,128)(2,1)}, u32[]{:S(2)}) copy-start(bf16[4,384,768]{2,1,0:T(8,128)(2,1)} %get-tuple-element.128) | copy-start | bytes 7077892
  91.2 18.3 %collective-permute-start.3 = (bf16[4,192,768]{2,1,0:T(8,128)(2,1)S(1)}, bf16[4,192,768]{2,1,0:T(8,128)(2,1)S(1)}, u32[]{:S(2)}, u32[]{:S(2)}) collective-permute-start(bf16[4,192,768]{2,1,0:T(8,128)(2,1)S(1)} %get-tuple-element.197), channel_id=1, source_target_pairs={{0,16},{4,12},{8,24},{12,4},{16,0},{20,28},{24,8},{28,20},{1,17},{... | collective-permute-start | bytes 3538952 | tf_op jit(solution)/shard_map/ppermute | solution.py:443
  92.8 16.8 %collective-permute-start.4 = (bf16[128,512]{1,0:T(8,128)(2,1)S(1)}, bf16[128,512]{1,0:T(8,128)(2,1)S(1)}, u32[]{:S(2)}, u32[]{:S(2)}) collective-permute-start(bf16[128,512]{1,0:T(8,128)(2,1)S(1)} %get-tuple-element.132), channel_id=1, source_target_pairs={{0,1},{1,0},{2,3},{3,2},{4,5},{5,4},{6,7},{7,6},{8,9},{9,8},{10,11... | collective-permute-start | bytes 393224 | tf_op jit(solution)/shard_map/ppermute | solution.py:502
  109.5 3.0 %copy-start.2 = (bf16[1024,768]{1,0:T(8,128)(2,1)}, bf16[1024,768]{1,0:T(8,128)(2,1)S(1)}, u32[]{:S(2)}) copy-start(bf16[1024,768]{1,0:T(8,128)(2,1)S(1)} %get-tuple-element.137.dq_ref) | copy-start | bytes 4718596
  109.5 3.0 %copy-start.4 = (bf16[1024,768]{1,0:T(8,128)(2,1)}, bf16[1024,768]{1,0:T(8,128)(2,1)S(1)}, u32[]{:S(2)}) copy-start(bf16[1024,768]{1,0:T(8,128)(2,1)S(1)} %get-tuple-element.142.o_ref) | copy-start | bytes 4718596
  109.5 8.7 %collective-permute-start.5 = (bf16[128,512]{1,0:T(8,128)(2,1)S(1)}, bf16[128,512]{1,0:T(8,128)(2,1)S(1)}, u32[]{:S(2)}, u32[]{:S(2)}) collective-permute-start(bf16[128,512]{1,0:T(8,128)(2,1)S(1)} %get-tuple-element.141), channel_id=1, source_target_pairs={{0,1},{1,0},{2,3},{3,2},{4,5},{5,4},{6,7},{7,6},{8,9},{9,8},{10,11... | collective-permute-start | bytes 393224 | tf_op jit(solution)/shard_map/ppermute | solution.py:506
  111.2 1.8 copy-start.1
  111.2 2.3 %copy-start.3 = (bf16[768,1024]{1,0:T(8,128)(2,1)S(1)}, bf16[768,1024]{1,0:T(8,128)(2,1)}, u32[]{:S(2)}) copy-start(bf16[768,1024]{1,0:T(8,128)(2,1)} %get-tuple-element.143.ai_ref) | copy-start | bytes 4718596
  113.5 4.8 %copy-start.5 = (f32[1024,256]{1,0:T(8,128)S(1)}, f32[1024,256]{1,0:T(8,128)}, u32[]{:S(2)}) copy-start(f32[1024,256]{1,0:T(8,128)} %get-tuple-element.123.tab_ref) | copy-start | bytes 3145732
  122.2 9.7 %collective-permute-start.6 = (bf16[4,96,1664]{2,1,0:T(8,128)(2,1)}, bf16[4,96,1664]{2,1,0:T(8,128)(2,1)}, u32[]{:S(2)}, u32[]{:S(2)}) collective-permute-start(bf16[4,96,1664]{2,1,0:T(8,128)(2,1)} %get-tuple-element.154), channel_id=1, source_target_pairs={{0,4},{4,0},{8,12},{12,8},{16,20},{20,16},{24,28},{28,24},{1,5},{5... | collective-permute-start | bytes 3833864 | tf_op jit(solution)/shard_map/ppermute | solution.py:443
  134.9 16.3 %collective-permute-start.7 = (bf16[4,48,1664]{2,1,0:T(8,128)(2,1)}, bf16[4,48,1664]{2,1,0:T(8,128)(2,1)}, u32[]{:S(2)}, u32[]{:S(2)}) collective-permute-start(bf16[4,48,1664]{2,1,0:T(8,128)(2,1)} %get-tuple-element.199), channel_id=1, source_target_pairs={{0,8},{4,20},{8,0},{12,28},{16,24},{20,4},{24,16},{28,12},{1,9},{5... | collective-permute-start | bytes 1916936 | tf_op jit(solution)/shard_map/ppermute | solution.py:443
  135.5 15.8 %collective-permute-start.8 = (bf16[2,192,768]{2,1,0:T(8,128)(2,1)}, bf16[2,192,768]{2,1,0:T(8,128)(2,1)}, u32[]{:S(2)}, u32[]{:S(2)}) collective-permute-start(bf16[2,192,768]{2,1,0:T(8,128)(2,1)} %get-tuple-element.149), channel_id=1, source_target_pairs={{0,1},{1,0},{2,3},{3,2},{4,5},{5,4},{6,7},{7,6},{8,9},{9,8},{10,11... | collective-permute-start | bytes 1769480 | tf_op jit(solution)/shard_map/ppermute | solution.py:443
  144.8 9.8 %copy-start.9 = (bf16[2,1,192,768]{3,2,1,0:T(8,128)(2,1)S(1)}, bf16[2,1,192,768]{3,2,1,0:T(8,128)(2,1)}, u32[]{:S(2)}) copy-start(bf16[2,1,192,768]{3,2,1,0:T(8,128)(2,1)} %get-tuple-element.200) | copy-start | bytes 1769476
  144.8 23.8 %collective-permute-start.10 = (f32[16,768]{1,0:T(8,128)}, f32[16,768]{1,0:T(8,128)}, u32[]{:S(2)}, u32[]{:S(2)}) collective-permute-start(f32[16,768]{1,0:T(8,128)} %get-tuple-element.163), channel_id=1, source_target_pairs={{0,4},{4,0},{8,12},{12,8},{16,20},{20,16},{24,28},{28,24},{1,5},{5... | collective-permute-start | bytes 147464 | tf_op jit(solution)/shard_map/ppermute | solution.py:537
  153.5 15.1 %collective-permute-start.9 = (bf16[4,24,1664]{2,1,0:T(8,128)(2,1)}, bf16[4,24,1664]{2,1,0:T(8,128)(2,1)}, u32[]{:S(2)}, u32[]{:S(2)}) collective-permute-start(bf16[4,24,1664]{2,1,0:T(8,128)(2,1)} %get-tuple-element.203), channel_id=1, source_target_pairs={{0,16},{4,12},{8,24},{12,4},{16,0},{20,28},{24,8},{28,20},{1,17},{... | collective-permute-start | bytes 958472 | tf_op jit(solution)/shard_map/ppermute | solution.py:443
  156.3 23.5 %collective-permute-start.12 = (bf16[192,768]{1,0:T(8,128)(2,1)}, bf16[192,768]{1,0:T(8,128)(2,1)}, u32[]{:S(2)}, u32[]{:S(2)}) collective-permute-start(bf16[192,768]{1,0:T(8,128)(2,1)} %fusion.7), channel_id=1, source_target_pairs={{0,2},{1,3},{2,0},{3,1},{4,6},{5,7},{6,4},{7,5},{8,10},{9,11},{10,... | collective-permute-start | bytes 884744 | tf_op jit(solution)/shard_map/ppermute | solution.py:443
  172.0 7.9 %collective-permute-start.11 = (bf16[2,24,1664]{2,1,0:T(8,128)(2,1)}, bf16[2,24,1664]{2,1,0:T(8,128)(2,1)}, u32[]{:S(2)}, u32[]{:S(2)}) collective-permute-start(bf16[2,24,1664]{2,1,0:T(8,128)(2,1)} %get-tuple-element.205), channel_id=1, source_target_pairs={{0,1},{1,0},{2,3},{3,2},{4,5},{5,4},{6,7},{7,6},{8,9},{9,8},{10,11... | collective-permute-start | bytes 479240 | tf_op jit(solution)/shard_map/ppermute | solution.py:443
  173.0 6.9 %collective-permute-start.13 = (f32[16,768]{1,0:T(8,128)}, f32[16,768]{1,0:T(8,128)}, u32[]{:S(2)}, u32[]{:S(2)}) collective-permute-start(f32[16,768]{1,0:T(8,128)} %add.153), channel_id=1, source_target_pairs={{0,8},{4,20},{8,0},{12,28},{16,24},{20,4},{24,16},{28,12},{1,9},{5... | collective-permute-start | bytes 147464 | tf_op jit(solution)/shard_map/ppermute | solution.py:537
  179.9 10.7 %copy-start.11 = (bf16[2,1,24,1664]{3,2,1,0:T(8,128)(2,1)S(1)}, bf16[2,1,24,1664]{3,2,1,0:T(8,128)(2,1)}, u32[]{:S(2)}) copy-start(bf16[2,1,24,1664]{3,2,1,0:T(8,128)(2,1)} %get-tuple-element.204) | copy-start | bytes 479236
  181.2 7.8 %collective-permute-start.15 = (bf16[192,768]{1,0:T(8,128)(2,1)S(1)}, bf16[192,768]{1,0:T(8,128)(2,1)S(1)}, u32[]{:S(2)}, u32[]{:S(2)}) collective-permute-start(bf16[192,768]{1,0:T(8,128)(2,1)S(1)} %fusion.3), channel_id=1, source_target_pairs={{0,16},{4,12},{8,24},{12,4},{16,0},{20,28},{24,8},{28,20},{1,17},{... | collective-permute-start | bytes 884744 | tf_op jit(solution)/shard_map/ppermute | solution.py:462
  182.7 6.2 %collective-permute-start.14 = (bf16[24,1664]{1,0:T(8,128)(2,1)S(1)}, bf16[24,1664]{1,0:T(8,128)(2,1)S(1)}, u32[]{:S(2)}, u32[]{:S(2)}) collective-permute-start(bf16[24,1664]{1,0:T(8,128)(2,1)S(1)} %fusion.13), channel_id=1, source_target_pairs={{0,2},{1,3},{2,0},{3,1},{4,6},{5,7},{6,4},{7,5},{8,10},{9,11},{10,... | collective-permute-start | bytes 239624 | tf_op jit(solution)/shard_map/ppermute | solution.py:443
  184.0 4.5 %collective-permute-start.16 = (f32[16,768]{1,0:T(8,128)S(1)}, f32[16,768]{1,0:T(8,128)S(1)}, u32[]{:S(2)}, u32[]{:S(2)}) collective-permute-start(f32[16,768]{1,0:T(8,128)S(1)} %add.159), channel_id=1, source_target_pairs={{0,16},{4,12},{8,24},{12,4},{16,0},{20,28},{24,8},{28,20},{1,17},{... | collective-permute-start | bytes 147464 | tf_op jit(solution)/shard_map/ppermute | solution.py:537
  189.0 13.3 %collective-permute-start.20 = (bf16[384,768]{1,0:T(8,128)(2,1)S(1)}, bf16[384,768]{1,0:T(8,128)(2,1)S(1)}, u32[]{:S(2)}, u32[]{:S(2)}) collective-permute-start(bf16[384,768]{1,0:T(8,128)(2,1)S(1)} %pad_maximum_fusion.1), channel_id=1, source_target_pairs={{0,8},{4,20},{8,0},{12,28},{16,24},{20,4},{24,16},{28,12},{1,9},{5... | collective-permute-start | bytes 1769480 | tf_op jit(solution)/shard_map/ppermute | solution.py:462
  191.5 5.4 %collective-permute-start.17 = (bf16[24,1664]{1,0:T(8,128)(2,1)S(1)}, bf16[24,1664]{1,0:T(8,128)(2,1)S(1)}, u32[]{:S(2)}, u32[]{:S(2)}) collective-permute-start(bf16[24,1664]{1,0:T(8,128)(2,1)S(1)} %fusion.10), channel_id=1, source_target_pairs={{0,16},{4,12},{8,24},{12,4},{16,0},{20,28},{24,8},{28,20},{1,17},{... | collective-permute-start | bytes 239624 | tf_op jit(solution)/shard_map/ppermute | solution.py:462
  192.6 4.1 %collective-permute-start.18 = (f32[16,768]{1,0:T(8,128)S(1)}, f32[16,768]{1,0:T(8,128)S(1)}, u32[]{:S(2)}, u32[]{:S(2)}) collective-permute-start(f32[16,768]{1,0:T(8,128)S(1)} %add.162), channel_id=1, source_target_pairs={{0,1},{1,0},{2,3},{3,2},{4,5},{5,4},{6,7},{7,6},{8,9},{9,8},{10,11... | collective-permute-start | bytes 147464 | tf_op jit(solution)/shard_map/ppermute | solution.py:537
  196.9 5.3 %collective-permute-start.19 = (bf16[48,1664]{1,0:T(8,128)(2,1)S(1)}, bf16[48,1664]{1,0:T(8,128)(2,1)S(1)}, u32[]{:S(2)}, u32[]{:S(2)}) collective-permute-start(bf16[48,1664]{1,0:T(8,128)(2,1)S(1)} %pad_maximum_fusion.3), channel_id=1, source_target_pairs={{0,8},{4,20},{8,0},{12,28},{16,24},{20,4},{24,16},{28,12},{1,9},{5... | collective-permute-start | bytes 479240 | tf_op jit(solution)/shard_map/ppermute | solution.py:462
  202.4 6.2 %collective-permute-start.21 = (bf16[768,768]{1,0:T(8,128)(2,1)S(1)}, bf16[768,768]{1,0:T(8,128)(2,1)S(1)}, u32[]{:S(2)}, u32[]{:S(2)}) collective-permute-start(bf16[768,768]{1,0:T(8,128)(2,1)S(1)} %pad_maximum_fusion.m_ref), channel_id=1, source_target_pairs={{0,4},{4,0},{8,12},{12,8},{16,20},{20,16},{24,28},{28,24},{1,5},{5... | collective-permute-start | bytes 3538952 | tf_op jit(solution)/shard_map/ppermute | solution.py:560
  202.5 6.1 %collective-permute-start.22 = (bf16[96,1664]{1,0:T(8,128)(2,1)S(1)}, bf16[96,1664]{1,0:T(8,128)(2,1)S(1)}, u32[]{:S(2)}, u32[]{:S(2)}) collective-permute-start(bf16[96,1664]{1,0:T(8,128)(2,1)S(1)} %pad_maximum_fusion.2.a_ref), channel_id=1, source_target_pairs={{0,4},{4,0},{8,12},{12,8},{16,20},{20,16},{24,28},{28,24},{1,5},{5... | collective-permute-start | bytes 958472 | tf_op jit(solution)/shard_map/ppermute | solution.py:561
  203.0 5.6 %collective-permute-start.23 = (f32[16,768]{1,0:T(8,128)S(1)}, f32[16,768]{1,0:T(8,128)S(1)}, u32[]{:S(2)}, u32[]{:S(2)}) collective-permute-start(f32[16,768]{1,0:T(8,128)S(1)} %add.163.s_ref), channel_id=1, source_target_pairs={{0,2},{1,3},{2,0},{3,1},{4,6},{5,7},{6,4},{7,5},{8,10},{9,11},{10,... | collective-permute-start | bytes 147464 | tf_op jit(solution)/shard_map/ppermute | solution.py:563
  (4 other events, 3.9 us)

commit v2 on v1

--- a/solution.py
+++ b/solution.py
@@ -345,7 +345,7 @@
     ws=pl.BlockSpec((D,D),(lambda j:(0,j)) if across else (lambda j:(j,0)))
     return pl.pallas_call(functools.partial(product_kernel,NT if across else NN),grid=(F//D,),
       in_specs=[pl.BlockSpec((N,D),lambda j:(0,j)),ws],out_specs=pl.BlockSpec((N,D),lambda j:(0,0)),out_shape=hs((N,D),F32),
-      cost_estimate=cost(4.8e9,1.4e7),compiler_params=params(1,None),name=name)(a,w)
+      cost_estimate=cost(4.8e9,1.4e7),compiler_params=params(1,26),name=name)(stay(a),stay(w))
 def postb_kernel(x_ref,g_ref,dq_ref,dkv_ref,c2_ref,wq_ref,wk_ref,wv_ref,vec_ref,qb_ref,hb_ref,kvb_ref,ig_ref,sm_ref):
     j=pl.program_id(0)
     @pl.when(j==0)
@@ -367,7 +367,7 @@
       in_specs=[rows_of(D,B)]*3+[rows_of(128,B),rows_of(D,B)]+[whole(a) for a in (wq,wk,wv,vec,qb,hb,kvb)],
       out_specs=[rows_of(D,B),pl.BlockSpec((16,D),lambda j:(0,0))],
       out_shape=[hs((N,D),F32),hs((16,D),F32)],
-      cost_estimate=cost(2e9,1.2e7),compiler_params=params(1,None),name="postb")(x,g,dq,dkv,c2,wq,wk,wv,vec,qb,hb,kvb)
+      cost_estimate=cost(2e9,1.2e7),compiler_params=params(1,26),name="postb")(*[stay(v) for v in (x,g,dq,dkv,c2,wq,wk,wv)],vec,qb,hb,kvb)
 def posta_kernel(x_ref,o_ref,mb_ref,wo_ref,vec_ref,lo_ref):
     lo_ref[...]=(x_ref[...].astype(F32)+(dotf(o_ref[...],wo_ref[...])+vec_ref[V_O:V_O+1,:])+(mb_ref[...]+vec_ref[V_D:V_D+1,:])).astype(BF)
 def posta(x,o,mb,wo,vec,B=256):
@@ -375,7 +375,7 @@
     return pl.pallas_call(posta_kernel,grid=(N//B,),
       in_specs=[rows_of(D,B)]*3+[whole(a) for a in (wo,vec)],
       out_specs=rows_of(D,B),out_shape=hs((N,D),BF),
-      cost_estimate=cost(2e9,9e6),compiler_params=params(1,None),name="posta")(x,o,mb,wo,vec)
+      cost_estimate=cost(2e9,9e6),compiler_params=params(1,20),name="posta")(*[stay(v) for v in (x,o,mb,wo)],vec)
 def final_kernel(sc,m_ref,mr_ref,a_ref,ar_ref,s_ref,sr_ref,w1_ref,w2_ref,wo_ref,wq_ref,wk_ref,wv_ref,
                  n1g_ref,n1b_ref,n2g_ref,n2b_ref,ob_ref,qb_ref,db_ref,hb_ref,kb_ref,vb_ref,kv_ref):
     W=w2_ref.shape[0]//2; D=m_ref.shape[1]; q=D//4; hr=a_ref.shape[0]; pr=hr//4; mr=m_ref.shape[0]//4
@@ -520,7 +520,7 @@
     small=None
     todo=[("dp",p) for _,p,_o in st]+[("sp",[(i,i^(1<<k)) for i in range(sp)]) for k in range(bits_of(sp))]
     c2=mb=ig=lo=sm=None
-    fill=["c2","ig","mb","lo"]
+    fill=["mb","c2","ig","lo"]
     held=1
     busy=True
     while True:

time: 214 us -> 199 us (0.930)
  other arithmetic: 19.3 us -> 5.62 us
  Pallas kernels: 142 us -> 139 us
    convert_element_type x9, other arithmetic: 14 us -> 2.52 us  [add(): return (a.astype(F32) + b.astype(F32)).astype(a.dtype)]
    ppermute x5, waiting for transfers between devices: 10.3 us -> 14.9 us  [on_device(): sr = lax.ppermute(small, axis, pairs)]
    ppermute x4, waiting for transfers between devices: 4.67 us -> 0.42 us  [gather_go(): self.recv = lax.ppermute(self.own, 'dp', self.st[self.left][1])]
    pallas_call x2, Pallas kernels: 19.4 us -> 16.1 us  [product(): pl.pallas_call(functools.partial(product_kernel, NT if across else NN), g...]
    add x4, other arithmetic: 2.29 us -> 0.03 us  [on_device(): small = small + got.pop(0)]
  transfers between devices with their start and end apart: 24 -> 24, of which waited for: 7 -> 7; matrix products, arithmetic and copies ran while one was open for 7% -> 2% of each run, Pallas kernels for 54% -> 56%
where the time goes in v2:
time: 199 us; the launch traced here: 198 us
  Pallas kernels  139 us (70%)
  starting transfers between devices  26.1 us (13%)
  waiting for transfers between devices  21.4 us (11%)
  other arithmetic  5.62 us (3%)
  local copies, waits for them, and re-layouts  4.84 us (2%)
    pallas_call x2, Pallas kernels, attn_part(): pl.pallas_call(body, grid=(count,), in_specs=ins, out_specs=specs, scratc...  47.8 us
    pallas_call x2, Pallas kernels, mlp_half(): pl.pallas_call(functools.partial(mlp_kernel, last, rows), grid_spec=pltpu...  39.9 us
    pallas_call x2, Pallas kernels, product(): pl.pallas_call(functools.partial(product_kernel, NT if across else NN), g...  16.1 us
    ppermute x5, waiting for transfers between devices, on_device(): sr = lax.ppermute(small, axis, pairs)  14.9 us
    ppermute x9, starting transfers between devices, go(): self.recv = lax.ppermute(self.send, axis, pairs)  10.7 us
    pallas_call x1, Pallas kernels, pre(): pl.pallas_call(pre_kernel, grid=(N // B,), in_specs=[row(D), row(D), col(...  9.12 us
    pallas_call x1, Pallas kernels, postb(): pl.pallas_call(postb_kernel, grid=(N // B,), in_specs=[rows_of(D, B)] * 3...  8.28 us
    ppermute x9, waiting for transfers between devices, go(): self.recv = lax.ppermute(self.send, axis, pairs)  6.12 us
  transfers between devices with their start and end apart: 24, of which 7 were waited for; matrix products, arithmetic and copies ran while one was open for 2% of the time, Pallas kernels for 56%

profile of v2, /device:TPU:0, one launch (start us, length us, event | category | flops | bytes accessed | tf_op | source)
XLA Modules:
  0.0 198.2 jit_solution(15554046474991842607)
XLA Ops:
  1.3 1.5 table.1.refs_7_.vec_ref
  2.8 20.3 %mlp_send.1 = (bf16[4,768,768]{2,1,0:T(8,128)(2,1)}, bf16[1024,3072]{1,0:T(8,128)(2,1)}, bf16[1024,3072]{1,0:T(8,128)(2,1)}, f32[2,1,768]{2,1,0:T(1,128)}, bf16[1024,768]{1,0:T(8,128)(2,1)}) custom-call(s32[2]{0:T(128)} %get-tuple-element.208.refs_0_, bf16[1024,768]{1,0:T(8,128)(2,1)} %bitcast.88, bf16[1024,768]{1,0:T(8,128)(2,1)} %bitcast.83, ...), custom_call_target="tpu_custom_call" | custom-call | flops 12562779136 | bytes 20000000 | tf_op jit(solution)/shard_map/mlp_send/pallas_call | solution.py:182
  26.1 9.1 %pre.1 = (bf16[6,1024,128]{2,1,0:T(8,128)(2,1)}, bf16[1024,128]{1,0:T(8,128)(2,1)}, bf16[6,1024,128]{2,1,0:T(8,128)(2,1)}, f32[1024,256]{1,0:T(8,128)}, bf16[768,1024]{1,0:T(8,128)(2,1)}) custom-call(bf16[1024,768]{1,0:T(8,128)(2,1)} %bitcast.89, bf16[1024,768]{1,0:T(8,128)(2,1)} %bitcast.84, f32[24,1024]{1,0:T(8,128)} %maximum_maximum_fusion.cs_ref, ...), custom_call_target="tpu_custom_call" | custom-call | flops 4000000000 | bytes 10000000 | tf_op jit(solution)/shard_map/pre/pallas_call | solution.py:87
  35.2 2.7 %collective-permute-start.1 = (bf16[1024,128]{1,0:T(8,128)(2,1)}, bf16[1024,128]{1,0:T(8,128)(2,1)}, u32[]{:S(2)}, u32[]{:S(2)}) collective-permute-start(bf16[1024,128]{1,0:T(8,128)(2,1)} %get-tuple-element.120.kv_ref), channel_id=1, source_target_pairs={{0,1},{1,0},{2,3},{3,2},{4,5},{5,4},{6,7},{7,6},{8,9},{9,8},{10,11... | collective-permute-start | bytes 786440 | tf_op jit(solution)/shard_map/ppermute | solution.py:492
  37.9 19.6 %mlp_keep.1 = (bf16[4,384,768]{2,1,0:T(8,128)(2,1)}, bf16[4,384,768]{2,1,0:T(8,128)(2,1)}, bf16[1024,3072]{1,0:T(8,128)(2,1)}, bf16[1024,3072]{1,0:T(8,128)(2,1)}, f32[4,768]{1,0:T(4,128)}) custom-call(s32[2]{0:T(128)} %get-tuple-element.209.refs_0_, bf16[1024,768]{1,0:T(8,128)(2,1)} %get-tuple-element.111.refs_1_, ...), custom_call_target="tpu_custom_call", output_to_operand_aliasing={{2}: (11, {}), {3}: (12, {})} | custom-call | flops 12562779136 | bytes 20000000 | tf_op jit(solution)/shard_map/mlp_keep/pallas_call | solution.py:182
  57.5 1.6 collective-permute-start.2
  59.0 31.5 %attn_a.1 = (bf16[1024,768]{1,0:T(8,128)(2,1)S(1)}, bf16[1024,768]{1,0:T(8,128)(2,1)S(1)}, f32[128,512]{1,0:T(8,128)S(1)}, bf16[128,512]{1,0:T(8,128)(2,1)S(1)}, f32[128,1024]{1,0:T(8,128)S(1)}) custom-call(bf16[6,1024,128]{2,1,0:T(8,128)(2,1)} %get-tuple-element.118.q_ref, bf16[6,1024,128]{2,1,0:T(8,128)(2,1)} %get-tuple-element.119.do_ref, ...), custom_call_target="tpu_custom_call" | custom-call | flops 32000000000 | bytes 5600000 | tf_op jit(solution)/shard_map/attn_a/pallas_call | solution.py:285
  91.1 1.6 collective-permute-start.3
  93.2 16.3 %attn_b.1 = (bf16[1024,768]{1,0:T(8,128)(2,1)S(1)}, bf16[1024,768]{1,0:T(8,128)(2,1)S(1)}, f32[128,512]{1,0:T(8,128)S(1)}, bf16[128,512]{1,0:T(8,128)(2,1)S(1)}) custom-call(bf16[6,1024,128]{2,1,0:T(8,128)(2,1)} %get-tuple-element.118.q_ref, bf16[6,1024,128]{2,1,0:T(8,128)(2,1)} %get-tuple-element.119.do_ref, ...), custom_call_target="tpu_custom_call", output_to_operand_aliasing={{0}: (6, {}), {1}: (7, {})} | custom-call | flops 16000000000 | bytes 2800000 | tf_op jit(solution)/shard_map/attn_b/pallas_call | solution.py:285
  109.5 1.6 collective-permute-start.5
  111.1 1.1 add_convert_fusion.4
  113.2 4.8 %wgrad.1 = (bf16[4,96,1664]{2,1,0:T(8,128)(2,1)S(1)}, bf16[4,96,1664]{2,1,0:T(8,128)(2,1)}, f32[1,768]{1,0:T(1,128)S(1)}) custom-call(s32[1]{0:T(128)} %bitcast.1.sc, bf16[1024,768]{1,0:T(8,128)(2,1)S(1)} %bitcast.87, bf16[1024,768]{1,0:T(8,128)(2,1)S(1)} %get-tuple-element.142.o_ref, bf16[1024,768]{1,0:T(8,128)(2,1)S(1)} %get-tuple-element.137.dq_ref, ...), custom_call_target="tpu_custom_call" | custom-call | flops 2600000000 | bytes 9000000 | tf_op jit(solution)/shard_map/wgrad/pallas_call | solution.py:315
  118.0 1.7 kvgrad.1
  120.3 8.0 %down.1.mb_ref = f32[1024,768]{1,0:T(8,128)S(1)} custom-call(bf16[1024,3072]{1,0:T(8,128)(2,1)} %get-tuple-element.156.a_ref, bf16[3072,768]{1,0:T(8,128)(2,1)} %w_ref.2), custom_call_target="tpu_custom_call" | custom-call | flops 4800000000 | bytes 14000000 | tf_op jit(solution)/shard_map/down/pallas_call | solution.py:346
  128.7 1.3 copy-done
  131.5 8.1 %back.1.c2_ref = f32[1024,768]{1,0:T(8,128)S(1)} custom-call(bf16[1024,3072]{1,0:T(8,128)(2,1)} %get-tuple-element.159.a_ref, bf16[768,3072]{1,0:T(8,128)(2,1)} %w_ref.3), custom_call_target="tpu_custom_call" | custom-call | flops 4800000000 | bytes 14000000 | tf_op jit(solution)/shard_map/back/pallas_call | solution.py:346
  139.6 1.7 copy-done.1
  141.3 4.7 %collective-permute-done.8 = bf16[2,192,768]{2,1,0:T(8,128)(2,1)S(1)} collective-permute-done((bf16[2,192,768]{2,1,0:T(8,128)(2,1)S(1)}, bf16[2,192,768]{2,1,0:T(8,128)(2,1)S(1)}, u32[]{:S(2)}, u32[]{:S(2)}) %collective-permute-start.8) | collective-permute-done | bytes 589856 | tf_op jit(solution)/shard_map/ppermute | solution.py:443
  146.2 1.1 collective-permute-start.9
  147.4 2.6 %collective-permute-start.11 = (bf16[192,768]{1,0:T(8,128)(2,1)S(1)}, bf16[192,768]{1,0:T(8,128)(2,1)S(1)}, u32[]{:S(2)}, u32[]{:S(2)}) collective-permute-start(bf16[192,768]{1,0:T(8,128)(2,1)S(1)} %fusion.7), channel_id=1, source_target_pairs={{0,2},{1,3},{2,0},{3,1},{4,6},{5,7},{6,4},{7,5},{8,10},{9,11},{10,... | collective-permute-start | bytes 884744 | tf_op jit(solution)/shard_map/ppermute | solution.py:443
  150.0 8.3 %postb.1 = (f32[1024,768]{1,0:T(8,128)}, f32[16,768]{1,0:T(8,128)S(1)}) custom-call(bf16[1024,768]{1,0:T(8,128)(2,1)} %bitcast.90, bf16[1024,768]{1,0:T(8,128)(2,1)} %bitcast.86, bf16[1024,768]{1,0:T(8,128)(2,1)} %copy-done.3, bf16[1024,128]{1,0:T(8,128)(2,1)} %copy-done.8, f32[1024,768]{1,0:T(8,128)} %copy-done.1, bf16[768,768]{1,0:T(8,128)(2,1)} %wq_ref.3, ...), custom_call_target="tpu_custom_call" | custom-call | flops 2000000000 | bytes 12000000 | tf_op jit(solution)/shard_map/postb/pallas_call | solution.py:366
  159.5 6.0 %posta.1 = bf16[1024,768]{1,0:T(8,128)(2,1)} custom-call(bf16[1024,768]{1,0:T(8,128)(2,1)} %bitcast.91, bf16[1024,768]{1,0:T(8,128)(2,1)} %copy-done.5, f32[1024,768]{1,0:T(8,128)} %copy-done, bf16[768,768]{1,0:T(8,128)(2,1)} %wo_ref.3, f32[12,768]{1,0:T(8,128)S(1)} %copy-done.7), custom_call_target="tpu_custom_call" | custom-call | flops 2000000000 | bytes 9000000 | tf_op jit(solution)/shard_map/posta/pallas_call | solution.py:375
  165.6 1.7 collective-permute-start.14
  167.4 1.2 collective-permute-start.13
  168.6 1.7 collective-permute-start.15
  170.3 2.4 %collective-permute-done.15 = f32[16,768]{1,0:T(8,128)S(1)} collective-permute-done((f32[16,768]{1,0:T(8,128)S(1)}, f32[16,768]{1,0:T(8,128)S(1)}, u32[]{:S(2)}, u32[]{:S(2)}) %collective-permute-start.15) | collective-permute-done | bytes 49184 | tf_op jit(solution)/shard_map/ppermute | solution.py:537
  172.7 1.4 collective-permute-done.13
  174.1 1.3 collective-permute-start.19
  177.6 4.4 %collective-permute-done.17 = f32[16,768]{1,0:T(8,128)S(1)} collective-permute-done((f32[16,768]{1,0:T(8,128)S(1)}, f32[16,768]{1,0:T(8,128)S(1)}, u32[]{:S(2)}, u32[]{:S(2)}) %collective-permute-start.17) | collective-permute-done | bytes 49184 | tf_op jit(solution)/shard_map/ppermute | solution.py:537
  183.8 3.1 %collective-permute-done.20 = f32[16,768]{1,0:T(8,128)S(1)} collective-permute-done((f32[16,768]{1,0:T(8,128)S(1)}, f32[16,768]{1,0:T(8,128)S(1)}, u32[]{:S(2)}, u32[]{:S(2)}) %collective-permute-start.20) | collective-permute-done | bytes 49184 | tf_op jit(solution)/shard_map/ppermute | solution.py:537
  189.0 5.1 %collective-permute-done.23.sr_ref = f32[16,768]{1,0:T(8,128)S(1)} collective-permute-done((f32[16,768]{1,0:T(8,128)S(1)}, f32[16,768]{1,0:T(8,128)S(1)}, u32[]{:S(2)}, u32[]{:S(2)}) %collective-permute-start.23) | collective-permute-done | bytes 49184 | tf_op jit(solution)/shard_map/ppermute | solution.py:563
  194.1 3.9 %final.1 = (f32[192,3072]{1,0:T(8,128)}, f32[768,768]{1,0:T(8,128)}, f32[192,768]{1,0:T(8,128)}, f32[192,768]{1,0:T(8,128)}, f32[64,192]{1,0:T(8,128)}, /*index=...) custom-call(s32[6]{0:T(128)S(1)} %stack.33.sc, ...), custom_call_target="tpu_custom_call" | custom-call | flops 1000000 | bytes 9000000 | tf_op jit(solution)/shard_map/final/pallas_call | solution.py:416
  (81 shorter events, 15.9 us)
Async XLA Ops:
  23.1 12.1 %collective-permute-start = (bf16[4,768,768]{2,1,0:T(8,128)(2,1)}, bf16[4,768,768]{2,1,0:T(8,128)(2,1)}, u32[]{:S(2)}, u32[]{:S(2)}) collective-permute-start(bf16[4,768,768]{2,1,0:T(8,128)(2,1)} %get-tuple-element.113), channel_id=1, source_target_pairs={{0,4},{4,0},{8,12},{12,8},{16,20},{20,16},{24,28},{28,24},{1,5},{5... | collective-permute-start | bytes 14155784 | tf_op jit(solution)/shard_map/ppermute | solution.py:483
  35.2 22.3 %collective-permute-start.1 = (bf16[1024,128]{1,0:T(8,128)(2,1)}, bf16[1024,128]{1,0:T(8,128)(2,1)}, u32[]{:S(2)}, u32[]{:S(2)}) collective-permute-start(bf16[1024,128]{1,0:T(8,128)(2,1)} %get-tuple-element.120.kv_ref), channel_id=1, source_target_pairs={{0,1},{1,0},{2,3},{3,2},{4,5},{5,4},{6,7},{7,6},{8,9},{9,8},{10,11... | collective-permute-start | bytes 786440 | tf_op jit(solution)/shard_map/ppermute | solution.py:492
  57.5 33.0 %collective-permute-start.2 = (bf16[4,384,768]{2,1,0:T(8,128)(2,1)}, bf16[4,384,768]{2,1,0:T(8,128)(2,1)S(1)}, u32[]{:S(2)}, u32[]{:S(2)}) collective-permute-start(bf16[4,384,768]{2,1,0:T(8,128)(2,1)} %get-tuple-element.129), channel_id=1, source_target_pairs={{0,8},{4,20},{8,0},{12,28},{16,24},{20,4},{24,16},{28,12},{1,9},{5... | collective-permute-start | bytes 7077896 | tf_op jit(solution)/shard_map/ppermute | solution.py:443
  59.0 31.5 %copy-start.10 = (bf16[4,384,768]{2,1,0:T(8,128)(2,1)S(1)}, bf16[4,384,768]{2,1,0:T(8,128)(2,1)}, u32[]{:S(2)}) copy-start(bf16[4,384,768]{2,1,0:T(8,128)(2,1)} %get-tuple-element.128) | copy-start | bytes 7077892
  91.1 18.4 %collective-permute-start.3 = (bf16[4,192,768]{2,1,0:T(8,128)(2,1)S(1)}, bf16[4,192,768]{2,1,0:T(8,128)(2,1)S(1)}, u32[]{:S(2)}, u32[]{:S(2)}) collective-permute-start(bf16[4,192,768]{2,1,0:T(8,128)(2,1)S(1)} %get-tuple-element.197), channel_id=1, source_target_pairs={{0,16},{4,12},{8,24},{12,4},{16,0},{20,28},{24,8},{28,20},{1,17},{... | collective-permute-start | bytes 3538952 | tf_op jit(solution)/shard_map/ppermute | solution.py:443
  92.7 16.8 %collective-permute-start.4 = (bf16[128,512]{1,0:T(8,128)(2,1)S(1)}, bf16[128,512]{1,0:T(8,128)(2,1)S(1)}, u32[]{:S(2)}, u32[]{:S(2)}) collective-permute-start(bf16[128,512]{1,0:T(8,128)(2,1)S(1)} %get-tuple-element.132), channel_id=1, source_target_pairs={{0,1},{1,0},{2,3},{3,2},{4,5},{5,4},{6,7},{7,6},{8,9},{9,8},{10,11... | collective-permute-start | bytes 393224 | tf_op jit(solution)/shard_map/ppermute | solution.py:502
  109.4 2.8 %copy-start.3 = (bf16[1024,768]{1,0:T(8,128)(2,1)}, bf16[1024,768]{1,0:T(8,128)(2,1)S(1)}, u32[]{:S(2)}) copy-start(bf16[1024,768]{1,0:T(8,128)(2,1)S(1)} %get-tuple-element.137.dq_ref) | copy-start | bytes 4718596
  109.4 2.8 %copy-start.5 = (bf16[1024,768]{1,0:T(8,128)(2,1)}, bf16[1024,768]{1,0:T(8,128)(2,1)S(1)}, u32[]{:S(2)}) copy-start(bf16[1024,768]{1,0:T(8,128)(2,1)S(1)} %get-tuple-element.142.o_ref) | copy-start | bytes 4718596
  109.5 8.5 %collective-permute-start.5 = (bf16[128,512]{1,0:T(8,128)(2,1)S(1)}, bf16[128,512]{1,0:T(8,128)(2,1)S(1)}, u32[]{:S(2)}, u32[]{:S(2)}) collective-permute-start(bf16[128,512]{1,0:T(8,128)(2,1)S(1)} %get-tuple-element.141), channel_id=1, source_target_pairs={{0,1},{1,0},{2,3},{3,2},{4,5},{5,4},{6,7},{7,6},{8,9},{9,8},{10,11... | collective-permute-start | bytes 393224 | tf_op jit(solution)/shard_map/ppermute | solution.py:506
  111.1 2.1 %copy-start.4 = (bf16[768,1024]{1,0:T(8,128)(2,1)S(1)}, bf16[768,1024]{1,0:T(8,128)(2,1)}, u32[]{:S(2)}) copy-start(bf16[768,1024]{1,0:T(8,128)(2,1)} %get-tuple-element.143.ai_ref) | copy-start | bytes 4718596
  113.2 4.8 %copy-start.6 = (f32[1024,256]{1,0:T(8,128)S(1)}, f32[1024,256]{1,0:T(8,128)}, u32[]{:S(2)}) copy-start(f32[1024,256]{1,0:T(8,128)} %get-tuple-element.123.tab_ref) | copy-start | bytes 3145732
  120.3 8.0 %collective-permute-start.6 = (bf16[4,96,1664]{2,1,0:T(8,128)(2,1)}, bf16[4,96,1664]{2,1,0:T(8,128)(2,1)S(1)}, u32[]{:S(2)}, u32[]{:S(2)}) collective-permute-start(bf16[4,96,1664]{2,1,0:T(8,128)(2,1)} %get-tuple-element.154), channel_id=1, source_target_pairs={{0,4},{4,0},{8,12},{12,8},{16,20},{20,16},{24,28},{28,24},{1,5},{5... | collective-permute-start | bytes 3833864 | tf_op jit(solution)/shard_map/ppermute | solution.py:443
  128.4 2.1 %copy-start.11 = (bf16[2,192,768]{2,1,0:T(8,128)(2,1)S(1)}, bf16[2,192,768]{2,1,0:T(8,128)(2,1)}, u32[]{:S(2)}) copy-start(bf16[2,192,768]{2,1,0:T(8,128)(2,1)} %get-tuple-element.149) | copy-start | bytes 1769476
  130.0 16.0 %collective-permute-start.7 = (bf16[4,48,1664]{2,1,0:T(8,128)(2,1)S(1)}, bf16[4,48,1664]{2,1,0:T(8,128)(2,1)S(1)}, u32[]{:S(2)}, u32[]{:S(2)}) collective-permute-start(bf16[4,48,1664]{2,1,0:T(8,128)(2,1)S(1)} %get-tuple-element.199), channel_id=1, source_target_pairs={{0,8},{4,20},{8,0},{12,28},{16,24},{20,4},{24,16},{28,12},{1,9},{5... | collective-permute-start | bytes 1916936 | tf_op jit(solution)/shard_map/ppermute | solution.py:443
  130.5 15.5 %collective-permute-start.8 = (bf16[2,192,768]{2,1,0:T(8,128)(2,1)S(1)}, bf16[2,192,768]{2,1,0:T(8,128)(2,1)S(1)}, u32[]{:S(2)}, u32[]{:S(2)}) collective-permute-start(bf16[2,192,768]{2,1,0:T(8,128)(2,1)S(1)} %copy-done.11), channel_id=1, source_target_pairs={{0,1},{1,0},{2,3},{3,2},{4,5},{5,4},{6,7},{7,6},{8,9},{9,8},{10,11... | collective-permute-start | bytes 1769480 | tf_op jit(solution)/shard_map/ppermute | solution.py:443
  146.0 4.0 %copy-start.7 = (f32[12,768]{1,0:T(8,128)S(1)}, f32[12,768]{1,0:T(8,128)}, u32[]{:S(2)}) copy-start(f32[12,768]{1,0:T(8,128)} %table.1.refs_7_.vec_ref) | copy-start | bytes 110596
  146.0 4.0 %copy-start.9 = (f32[4,768]{1,0:T(4,128)S(1)}, f32[4,768]{1,0:T(4,128)}, u32[]{:S(2)}) copy-start(f32[4,768]{1,0:T(4,128)} %get-tuple-element.117.hb_ref) | copy-start | bytes 36868
  146.2 12.1 %collective-permute-start.9 = (bf16[4,24,1664]{2,1,0:T(8,128)(2,1)S(1)}, bf16[4,24,1664]{2,1,0:T(8,128)(2,1)S(1)}, u32[]{:S(2)}, u32[]{:S(2)}) collective-permute-start(bf16[4,24,1664]{2,1,0:T(8,128)(2,1)S(1)} %get-tuple-element.203), channel_id=1, source_target_pairs={{0,16},{4,12},{8,24},{12,4},{16,0},{20,28},{24,8},{28,20},{1,17},{... | collective-permute-start | bytes 958472 | tf_op jit(solution)/shard_map/ppermute | solution.py:443
  147.4 18.1 %collective-permute-start.11 = (bf16[192,768]{1,0:T(8,128)(2,1)S(1)}, bf16[192,768]{1,0:T(8,128)(2,1)S(1)}, u32[]{:S(2)}, u32[]{:S(2)}) collective-permute-start(bf16[192,768]{1,0:T(8,128)(2,1)S(1)} %fusion.7), channel_id=1, source_target_pairs={{0,2},{1,3},{2,0},{3,1},{4,6},{5,7},{6,4},{7,5},{8,10},{9,11},{10,... | collective-permute-start | bytes 884744 | tf_op jit(solution)/shard_map/ppermute | solution.py:443
  158.3 7.2 %collective-permute-start.12 = (f32[16,768]{1,0:T(8,128)S(1)}, f32[16,768]{1,0:T(8,128)S(1)}, u32[]{:S(2)}, u32[]{:S(2)}) collective-permute-start(f32[16,768]{1,0:T(8,128)S(1)} %get-tuple-element.167), channel_id=1, source_target_pairs={{0,4},{4,0},{8,12},{12,8},{16,20},{20,16},{24,28},{28,24},{1,5},{5... | collective-permute-start | bytes 147464 | tf_op jit(solution)/shard_map/ppermute | solution.py:537
  158.4 7.1 %collective-permute-start.10 = (bf16[2,24,1664]{2,1,0:T(8,128)(2,1)S(1)}, bf16[2,24,1664]{2,1,0:T(8,128)(2,1)S(1)}, u32[]{:S(2)}, u32[]{:S(2)}) collective-permute-start(bf16[2,24,1664]{2,1,0:T(8,128)(2,1)S(1)} %get-tuple-element.205), channel_id=1, source_target_pairs={{0,1},{1,0},{2,3},{3,2},{4,5},{5,4},{6,7},{7,6},{8,9},{9,8},{10,11... | collective-permute-start | bytes 479240 | tf_op jit(solution)/shard_map/ppermute | solution.py:443
  165.6 8.5 %collective-permute-start.14 = (bf16[192,768]{1,0:T(8,128)(2,1)S(1)}, bf16[192,768]{1,0:T(8,128)(2,1)S(1)}, u32[]{:S(2)}, u32[]{:S(2)}) collective-permute-start(bf16[192,768]{1,0:T(8,128)(2,1)S(1)} %fusion.3), channel_id=1, source_target_pairs={{0,16},{4,12},{8,24},{12,4},{16,0},{20,28},{24,8},{28,20},{1,17},{... | collective-permute-start | bytes 884744 | tf_op jit(solution)/shard_map/ppermute | solution.py:462
  167.4 6.7 %collective-permute-start.13 = (bf16[24,1664]{1,0:T(8,128)(2,1)S(1)}, bf16[24,1664]{1,0:T(8,128)(2,1)S(1)}, u32[]{:S(2)}, u32[]{:S(2)}) collective-permute-start(bf16[24,1664]{1,0:T(8,128)(2,1)S(1)} %fusion.13), channel_id=1, source_target_pairs={{0,2},{1,3},{2,0},{3,1},{4,6},{5,7},{6,4},{7,5},{8,10},{9,11},{10,... | collective-permute-start | bytes 239624 | tf_op jit(solution)/shard_map/ppermute | solution.py:443
  168.6 4.1 %collective-permute-start.15 = (f32[16,768]{1,0:T(8,128)S(1)}, f32[16,768]{1,0:T(8,128)S(1)}, u32[]{:S(2)}, u32[]{:S(2)}) collective-permute-start(f32[16,768]{1,0:T(8,128)S(1)} %add.158), channel_id=1, source_target_pairs={{0,8},{4,20},{8,0},{12,28},{16,24},{20,4},{24,16},{28,12},{1,9},{5... | collective-permute-start | bytes 147464 | tf_op jit(solution)/shard_map/ppermute | solution.py:537
  174.1 13.2 %collective-permute-start.19 = (bf16[384,768]{1,0:T(8,128)(2,1)S(1)}, bf16[384,768]{1,0:T(8,128)(2,1)S(1)}, u32[]{:S(2)}, u32[]{:S(2)}) collective-permute-start(bf16[384,768]{1,0:T(8,128)(2,1)S(1)} %pad_maximum_fusion.1), channel_id=1, source_target_pairs={{0,8},{4,20},{8,0},{12,28},{16,24},{20,4},{24,16},{28,12},{1,9},{5... | collective-permute-start | bytes 1769480 | tf_op jit(solution)/shard_map/ppermute | solution.py:462
  175.5 6.5 %collective-permute-start.16 = (bf16[24,1664]{1,0:T(8,128)(2,1)S(1)}, bf16[24,1664]{1,0:T(8,128)(2,1)S(1)}, u32[]{:S(2)}, u32[]{:S(2)}) collective-permute-start(bf16[24,1664]{1,0:T(8,128)(2,1)S(1)} %fusion.10), channel_id=1, source_target_pairs={{0,16},{4,12},{8,24},{12,4},{16,0},{20,28},{24,8},{28,20},{1,17},{... | collective-permute-start | bytes 239624 | tf_op jit(solution)/shard_map/ppermute | solution.py:462
  176.5 5.4 %collective-permute-start.17 = (f32[16,768]{1,0:T(8,128)S(1)}, f32[16,768]{1,0:T(8,128)S(1)}, u32[]{:S(2)}, u32[]{:S(2)}) collective-permute-start(f32[16,768]{1,0:T(8,128)S(1)} %add.161), channel_id=1, source_target_pairs={{0,16},{4,12},{8,24},{12,4},{16,0},{20,28},{24,8},{28,20},{1,17},{... | collective-permute-start | bytes 147464 | tf_op jit(solution)/shard_map/ppermute | solution.py:537
  182.0 5.3 %collective-permute-start.18 = (bf16[48,1664]{1,0:T(8,128)(2,1)S(1)}, bf16[48,1664]{1,0:T(8,128)(2,1)S(1)}, u32[]{:S(2)}, u32[]{:S(2)}) collective-permute-start(bf16[48,1664]{1,0:T(8,128)(2,1)S(1)} %pad_maximum_fusion.3), channel_id=1, source_target_pairs={{0,8},{4,20},{8,0},{12,28},{16,24},{20,4},{24,16},{28,12},{1,9},{5... | collective-permute-start | bytes 479240 | tf_op jit(solution)/shard_map/ppermute | solution.py:462
  182.8 4.1 %collective-permute-start.20 = (f32[16,768]{1,0:T(8,128)S(1)}, f32[16,768]{1,0:T(8,128)S(1)}, u32[]{:S(2)}, u32[]{:S(2)}) collective-permute-start(f32[16,768]{1,0:T(8,128)S(1)} %add.162), channel_id=1, source_target_pairs={{0,1},{1,0},{2,3},{3,2},{4,5},{5,4},{6,7},{7,6},{8,9},{9,8},{10,11... | collective-permute-start | bytes 147464 | tf_op jit(solution)/shard_map/ppermute | solution.py:537
  187.4 6.7 %collective-permute-start.21 = (bf16[768,768]{1,0:T(8,128)(2,1)S(1)}, bf16[768,768]{1,0:T(8,128)(2,1)S(1)}, u32[]{:S(2)}, u32[]{:S(2)}) collective-permute-start(bf16[768,768]{1,0:T(8,128)(2,1)S(1)} %pad_maximum_fusion.m_ref), channel_id=1, source_target_pairs={{0,4},{4,0},{8,12},{12,8},{16,20},{20,16},{24,28},{28,24},{1,5},{5... | collective-permute-start | bytes 3538952 | tf_op jit(solution)/shard_map/ppermute | solution.py:560
  187.5 6.6 %collective-permute-start.22 = (bf16[96,1664]{1,0:T(8,128)(2,1)S(1)}, bf16[96,1664]{1,0:T(8,128)(2,1)S(1)}, u32[]{:S(2)}, u32[]{:S(2)}) collective-permute-start(bf16[96,1664]{1,0:T(8,128)(2,1)S(1)} %pad_maximum_fusion.2.a_ref), channel_id=1, source_target_pairs={{0,4},{4,0},{8,12},{12,8},{16,20},{20,16},{24,28},{28,24},{1,5},{5... | collective-permute-start | bytes 958472 | tf_op jit(solution)/shard_map/ppermute | solution.py:561
  188.1 6.0 %collective-permute-start.23 = (f32[16,768]{1,0:T(8,128)S(1)}, f32[16,768]{1,0:T(8,128)S(1)}, u32[]{:S(2)}, u32[]{:S(2)}) collective-permute-start(f32[16,768]{1,0:T(8,128)S(1)} %add.163.s_ref), channel_id=1, source_target_pairs={{0,2},{1,3},{2,0},{3,1},{4,6},{5,7},{6,4},{7,5},{8,10},{9,11},{10,... | collective-permute-start | bytes 147464 | tf_op jit(solution)/shard_map/ppermute | solution.py:563
  (4 other events, 5.6 us)

commit v3 on v2

--- a/solution.py
+++ b/solution.py
@@ -520,7 +520,7 @@
     small=None
     todo=[("dp",p) for _,p,_o in st]+[("sp",[(i,i^(1<<k)) for i in range(sp)]) for k in range(bits_of(sp))]
     c2=mb=ig=lo=sm=None
-    fill=["mb","c2","ig","lo"]
+    fill=["","c2","ig","mb","lo"]
     held=1
     busy=True
     while True:

time: 199 us -> 196 us (0.985)
    ppermute x5, waiting for transfers between devices: 14.9 us -> 11 us  [on_device(): sr = lax.ppermute(small, axis, pairs)]
  transfers between devices with their start and end apart: 24 -> 24, of which waited for: 7 -> 7; matrix products, arithmetic and copies ran while one was open for 2% -> 2% of each run, Pallas kernels for 56% -> 57%
where the time goes in v3:
time: 196 us
  Pallas kernels  139 us (71%)
  starting transfers between devices  24.8 us (13%)
  waiting for transfers between devices  19.6 us (10%)
  other arithmetic  5.63 us (3%)
  local copies, waits for them, and re-layouts  5.38 us (3%)
    pallas_call x2, Pallas kernels, attn_part(): pl.pallas_call(body, grid=(count,), in_specs=ins, out_specs=specs, scratc...  47.8 us
    pallas_call x2, Pallas kernels, mlp_half(): pl.pallas_call(functools.partial(mlp_kernel, last, rows), grid_spec=pltpu...  39.9 us
    pallas_call x2, Pallas kernels, product(): pl.pallas_call(functools.partial(product_kernel, NT if across else NN), g...  16.1 us
    ppermute x5, waiting for transfers between devices, on_device(): sr = lax.ppermute(small, axis, pairs)  11 us
    ppermute x9, starting transfers between devices, go(): self.recv = lax.ppermute(self.send, axis, pairs)  9.96 us
    pallas_call x1, Pallas kernels, pre(): pl.pallas_call(pre_kernel, grid=(N // B,), in_specs=[row(D), row(D), col(...  9.12 us
    pallas_call x1, Pallas kernels, postb(): pl.pallas_call(postb_kernel, grid=(N // B,), in_specs=[rows_of(D, B)] * 3...  8.51 us
    ppermute x9, waiting for transfers between devices, go(): self.recv = lax.ppermute(self.send, axis, pairs)  8.01 us
  transfers between devices with their start and end apart: 24, of which 7 were waited for; matrix products, arithmetic and copies ran while one was open for 2% of the time, Pallas kernels for 57%

profile of v3, /device:TPU:0, one launch (start us, length us, event | category | flops | bytes accessed | tf_op | source)
XLA Modules:
  0.0 195.8 jit_solution(12234984076299496552)
XLA Ops:
  1.3 1.5 table.1.refs_7_.vec_ref
  2.8 20.3 %mlp_send.1 = (bf16[4,768,768]{2,1,0:T(8,128)(2,1)}, bf16[1024,3072]{1,0:T(8,128)(2,1)}, bf16[1024,3072]{1,0:T(8,128)(2,1)}, f32[2,1,768]{2,1,0:T(1,128)}, bf16[1024,768]{1,0:T(8,128)(2,1)}) custom-call(s32[2]{0:T(128)} %get-tuple-element.206.refs_0_, bf16[1024,768]{1,0:T(8,128)(2,1)} %bitcast.88, bf16[1024,768]{1,0:T(8,128)(2,1)} %bitcast.83, ...), custom_call_target="tpu_custom_call" | custom-call | flops 12562779136 | bytes 20000000 | tf_op jit(solution)/shard_map/mlp_send/pallas_call | solution.py:182
  26.1 9.1 %pre.1 = (bf16[6,1024,128]{2,1,0:T(8,128)(2,1)}, bf16[1024,128]{1,0:T(8,128)(2,1)}, bf16[6,1024,128]{2,1,0:T(8,128)(2,1)}, f32[1024,256]{1,0:T(8,128)}, bf16[768,1024]{1,0:T(8,128)(2,1)}) custom-call(bf16[1024,768]{1,0:T(8,128)(2,1)} %bitcast.89, bf16[1024,768]{1,0:T(8,128)(2,1)} %bitcast.84, f32[24,1024]{1,0:T(8,128)} %maximum_maximum_fusion.cs_ref, ...), custom_call_target="tpu_custom_call" | custom-call | flops 4000000000 | bytes 10000000 | tf_op jit(solution)/shard_map/pre/pallas_call | solution.py:87
  35.2 2.7 %collective-permute-start.1 = (bf16[1024,128]{1,0:T(8,128)(2,1)}, bf16[1024,128]{1,0:T(8,128)(2,1)}, u32[]{:S(2)}, u32[]{:S(2)}) collective-permute-start(bf16[1024,128]{1,0:T(8,128)(2,1)} %get-tuple-element.119.kv_ref), channel_id=1, source_target_pairs={{0,1},{1,0},{2,3},{3,2},{4,5},{5,4},{6,7},{7,6},{8,9},{9,8},{10,11... | collective-permute-start | bytes 786440 | tf_op jit(solution)/shard_map/ppermute | solution.py:492
  37.9 19.6 %mlp_keep.1 = (bf16[4,384,768]{2,1,0:T(8,128)(2,1)}, bf16[4,384,768]{2,1,0:T(8,128)(2,1)}, bf16[1024,3072]{1,0:T(8,128)(2,1)}, bf16[1024,3072]{1,0:T(8,128)(2,1)}, f32[4,768]{1,0:T(4,128)}) custom-call(s32[2]{0:T(128)} %get-tuple-element.207.refs_0_, bf16[1024,768]{1,0:T(8,128)(2,1)} %get-tuple-element.110.refs_1_, ...), custom_call_target="tpu_custom_call", output_to_operand_aliasing={{2}: (11, {}), {3}: (12, {})} | custom-call | flops 12562779136 | bytes 20000000 | tf_op jit(solution)/shard_map/mlp_keep/pallas_call | solution.py:182
  57.5 1.6 collective-permute-start.2
  59.0 31.5 %attn_a.1 = (bf16[1024,768]{1,0:T(8,128)(2,1)S(1)}, bf16[1024,768]{1,0:T(8,128)(2,1)S(1)}, f32[128,512]{1,0:T(8,128)S(1)}, bf16[128,512]{1,0:T(8,128)(2,1)S(1)}, f32[128,1024]{1,0:T(8,128)S(1)}) custom-call(bf16[6,1024,128]{2,1,0:T(8,128)(2,1)} %get-tuple-element.117.q_ref, bf16[6,1024,128]{2,1,0:T(8,128)(2,1)} %get-tuple-element.118.do_ref, ...), custom_call_target="tpu_custom_call" | custom-call | flops 32000000000 | bytes 5600000 | tf_op jit(solution)/shard_map/attn_a/pallas_call | solution.py:285
  91.1 1.6 collective-permute-start.3
  93.2 16.3 %attn_b.1 = (bf16[1024,768]{1,0:T(8,128)(2,1)S(1)}, bf16[1024,768]{1,0:T(8,128)(2,1)S(1)}, f32[128,512]{1,0:T(8,128)S(1)}, bf16[128,512]{1,0:T(8,128)(2,1)S(1)}) custom-call(bf16[6,1024,128]{2,1,0:T(8,128)(2,1)} %get-tuple-element.117.q_ref, bf16[6,1024,128]{2,1,0:T(8,128)(2,1)} %get-tuple-element.118.do_ref, ...), custom_call_target="tpu_custom_call", output_to_operand_aliasing={{0}: (6, {}), {1}: (7, {})} | custom-call | flops 16000000000 | bytes 2800000 | tf_op jit(solution)/shard_map/attn_b/pallas_call | solution.py:285
  109.5 1.6 collective-permute-start.5
  111.1 1.1 add_convert_fusion.4
  113.2 4.8 %wgrad.1 = (bf16[4,96,1664]{2,1,0:T(8,128)(2,1)S(1)}, bf16[4,96,1664]{2,1,0:T(8,128)(2,1)}, f32[1,768]{1,0:T(1,128)S(1)}) custom-call(s32[1]{0:T(128)} %bitcast.1.sc, bf16[1024,768]{1,0:T(8,128)(2,1)S(1)} %bitcast.87, bf16[1024,768]{1,0:T(8,128)(2,1)S(1)} %get-tuple-element.141.o_ref, bf16[1024,768]{1,0:T(8,128)(2,1)S(1)} %get-tuple-element.136.dq_ref, ...), custom_call_target="tpu_custom_call" | custom-call | flops 2600000000 | bytes 9000000 | tf_op jit(solution)/shard_map/wgrad/pallas_call | solution.py:315
  118.0 1.7 kvgrad.1
  120.3 3.2 %collective-permute-done.6 = bf16[4,96,1664]{2,1,0:T(8,128)(2,1)S(1)} collective-permute-done((bf16[4,96,1664]{2,1,0:T(8,128)(2,1)}, bf16[4,96,1664]{2,1,0:T(8,128)(2,1)S(1)}, u32[]{:S(2)}, u32[]{:S(2)}) %collective-permute-start.6) | collective-permute-done | bytes 1277984 | tf_op jit(solution)/shard_map/ppermute | solution.py:443
  125.6 8.1 %back.1.c2_ref = f32[1024,768]{1,0:T(8,128)S(1)} custom-call(bf16[1024,3072]{1,0:T(8,128)(2,1)} %get-tuple-element.155.a_ref, bf16[768,3072]{1,0:T(8,128)(2,1)} %w_ref.2), custom_call_target="tpu_custom_call" | custom-call | flops 4800000000 | bytes 14000000 | tf_op jit(solution)/shard_map/back/pallas_call | solution.py:346
  133.7 1.7 copy-done.1
  135.4 4.5 %collective-permute-done.8 = bf16[2,192,768]{2,1,0:T(8,128)(2,1)S(1)} collective-permute-done((bf16[2,192,768]{2,1,0:T(8,128)(2,1)S(1)}, bf16[2,192,768]{2,1,0:T(8,128)(2,1)S(1)}, u32[]{:S(2)}, u32[]{:S(2)}) %collective-permute-start.8) | collective-permute-done | bytes 589856 | tf_op jit(solution)/shard_map/ppermute | solution.py:443
  140.2 1.1 collective-permute-start.9
  141.4 2.7 %collective-permute-start.11 = (bf16[192,768]{1,0:T(8,128)(2,1)S(1)}, bf16[192,768]{1,0:T(8,128)(2,1)S(1)}, u32[]{:S(2)}, u32[]{:S(2)}) collective-permute-start(bf16[192,768]{1,0:T(8,128)(2,1)S(1)} %fusion.7), channel_id=1, source_target_pairs={{0,2},{1,3},{2,0},{3,1},{4,6},{5,7},{6,4},{7,5},{8,10},{9,11},{10,... | collective-permute-start | bytes 884744 | tf_op jit(solution)/shard_map/ppermute | solution.py:443
  144.0 8.5 %postb.1 = (f32[1024,768]{1,0:T(8,128)}, f32[16,768]{1,0:T(8,128)S(1)}) custom-call(bf16[1024,768]{1,0:T(8,128)(2,1)} %bitcast.90, bf16[1024,768]{1,0:T(8,128)(2,1)} %bitcast.86, bf16[1024,768]{1,0:T(8,128)(2,1)} %copy-done.3, bf16[1024,128]{1,0:T(8,128)(2,1)} %copy-done.8, f32[1024,768]{1,0:T(8,128)} %copy-done.1, bf16[768,768]{1,0:T(8,128)(2,1)} %wq_ref.3, ...), custom_call_target="tpu_custom_call" | custom-call | flops 2000000000 | bytes 12000000 | tf_op jit(solution)/shard_map/postb/pallas_call | solution.py:366
  152.7 1.1 collective-permute-start.10
  153.7 8.0 %down.1.mb_ref = f32[1024,768]{1,0:T(8,128)S(1)} custom-call(bf16[1024,3072]{1,0:T(8,128)(2,1)} %get-tuple-element.165.a_ref, bf16[3072,768]{1,0:T(8,128)(2,1)} %w_ref.3), custom_call_target="tpu_custom_call" | custom-call | flops 4800000000 | bytes 14000000 | tf_op jit(solution)/shard_map/down/pallas_call | solution.py:346
  161.8 1.6 copy-done
  163.5 1.0 collective-permute-start.14
  165.5 6.0 %posta.1 = bf16[1024,768]{1,0:T(8,128)(2,1)} custom-call(bf16[1024,768]{1,0:T(8,128)(2,1)} %bitcast.91, bf16[1024,768]{1,0:T(8,128)(2,1)} %copy-done.5, f32[1024,768]{1,0:T(8,128)} %copy-done, bf16[768,768]{1,0:T(8,128)(2,1)} %wo_ref.3, f32[12,768]{1,0:T(8,128)S(1)} %copy-done.7), custom_call_target="tpu_custom_call" | custom-call | flops 2000000000 | bytes 9000000 | tf_op jit(solution)/shard_map/posta/pallas_call | solution.py:375
  171.8 1.6 collective-permute-start.19
  173.4 1.1 collective-permute-start.16
  175.5 4.4 %collective-permute-done.17 = f32[16,768]{1,0:T(8,128)S(1)} collective-permute-done((f32[16,768]{1,0:T(8,128)S(1)}, f32[16,768]{1,0:T(8,128)S(1)}, u32[]{:S(2)}, u32[]{:S(2)}) %collective-permute-start.17) | collective-permute-done | bytes 49184 | tf_op jit(solution)/shard_map/ppermute | solution.py:537
  181.3 3.3 %collective-permute-done.20 = f32[16,768]{1,0:T(8,128)S(1)} collective-permute-done((f32[16,768]{1,0:T(8,128)S(1)}, f32[16,768]{1,0:T(8,128)S(1)}, u32[]{:S(2)}, u32[]{:S(2)}) %collective-permute-start.20) | collective-permute-done | bytes 49184 | tf_op jit(solution)/shard_map/ppermute | solution.py:537
  186.0 2.3 %collective-permute-start.23 = (f32[16,768]{1,0:T(8,128)S(1)}, f32[16,768]{1,0:T(8,128)S(1)}, u32[]{:S(2)}, u32[]{:S(2)}) collective-permute-start(f32[16,768]{1,0:T(8,128)S(1)} %add.163.s_ref), channel_id=1, source_target_pairs={{0,2},{1,3},{2,0},{3,1},{4,6},{5,7},{6,4},{7,5},{8,10},{9,11},{10,... | collective-permute-start | bytes 147464 | tf_op jit(solution)/shard_map/ppermute | solution.py:563
  188.4 3.3 %collective-permute-done.23.sr_ref = f32[16,768]{1,0:T(8,128)S(1)} collective-permute-done((f32[16,768]{1,0:T(8,128)S(1)}, f32[16,768]{1,0:T(8,128)S(1)}, u32[]{:S(2)}, u32[]{:S(2)}) %collective-permute-start.23) | collective-permute-done | bytes 49184 | tf_op jit(solution)/shard_map/ppermute | solution.py:563
  191.7 3.9 %final.1 = (f32[192,3072]{1,0:T(8,128)}, f32[768,768]{1,0:T(8,128)}, f32[192,768]{1,0:T(8,128)}, f32[192,768]{1,0:T(8,128)}, f32[64,192]{1,0:T(8,128)}, /*index=...) custom-call(s32[6]{0:T(128)S(1)} %stack.33.sc, ...), custom_call_target="tpu_custom_call" | custom-call | flops 1000000 | bytes 9000000 | tf_op jit(solution)/shard_map/final/pallas_call | solution.py:416
  (81 shorter events, 14.0 us)
Async XLA Ops:
  23.1 12.1 %collective-permute-start = (bf16[4,768,768]{2,1,0:T(8,128)(2,1)}, bf16[4,768,768]{2,1,0:T(8,128)(2,1)}, u32[]{:S(2)}, u32[]{:S(2)}) collective-permute-start(bf16[4,768,768]{2,1,0:T(8,128)(2,1)} %get-tuple-element.112), channel_id=1, source_target_pairs={{0,4},{4,0},{8,12},{12,8},{16,20},{20,16},{24,28},{28,24},{1,5},{5... | collective-permute-start | bytes 14155784 | tf_op jit(solution)/shard_map/ppermute | solution.py:483
  35.2 22.3 %collective-permute-start.1 = (bf16[1024,128]{1,0:T(8,128)(2,1)}, bf16[1024,128]{1,0:T(8,128)(2,1)}, u32[]{:S(2)}, u32[]{:S(2)}) collective-permute-start(bf16[1024,128]{1,0:T(8,128)(2,1)} %get-tuple-element.119.kv_ref), channel_id=1, source_target_pairs={{0,1},{1,0},{2,3},{3,2},{4,5},{5,4},{6,7},{7,6},{8,9},{9,8},{10,11... | collective-permute-start | bytes 786440 | tf_op jit(solution)/shard_map/ppermute | solution.py:492
  57.5 33.0 %collective-permute-start.2 = (bf16[4,384,768]{2,1,0:T(8,128)(2,1)}, bf16[4,384,768]{2,1,0:T(8,128)(2,1)S(1)}, u32[]{:S(2)}, u32[]{:S(2)}) collective-permute-start(bf16[4,384,768]{2,1,0:T(8,128)(2,1)} %get-tuple-element.128), channel_id=1, source_target_pairs={{0,8},{4,20},{8,0},{12,28},{16,24},{20,4},{24,16},{28,12},{1,9},{5... | collective-permute-start | bytes 7077896 | tf_op jit(solution)/shard_map/ppermute | solution.py:443
  59.0 31.5 %copy-start.10 = (bf16[4,384,768]{2,1,0:T(8,128)(2,1)S(1)}, bf16[4,384,768]{2,1,0:T(8,128)(2,1)}, u32[]{:S(2)}) copy-start(bf16[4,384,768]{2,1,0:T(8,128)(2,1)} %get-tuple-element.127) | copy-start | bytes 7077892
  91.1 18.4 %collective-permute-start.3 = (bf16[4,192,768]{2,1,0:T(8,128)(2,1)S(1)}, bf16[4,192,768]{2,1,0:T(8,128)(2,1)S(1)}, u32[]{:S(2)}, u32[]{:S(2)}) collective-permute-start(bf16[4,192,768]{2,1,0:T(8,128)(2,1)S(1)} %get-tuple-element.195), channel_id=1, source_target_pairs={{0,16},{4,12},{8,24},{12,4},{16,0},{20,28},{24,8},{28,20},{1,17},{... | collective-permute-start | bytes 3538952 | tf_op jit(solution)/shard_map/ppermute | solution.py:443
  92.7 16.8 %collective-permute-start.4 = (bf16[128,512]{1,0:T(8,128)(2,1)S(1)}, bf16[128,512]{1,0:T(8,128)(2,1)S(1)}, u32[]{:S(2)}, u32[]{:S(2)}) collective-permute-start(bf16[128,512]{1,0:T(8,128)(2,1)S(1)} %get-tuple-element.131), channel_id=1, source_target_pairs={{0,1},{1,0},{2,3},{3,2},{4,5},{5,4},{6,7},{7,6},{8,9},{9,8},{10,11... | collective-permute-start | bytes 393224 | tf_op jit(solution)/shard_map/ppermute | solution.py:502
  109.4 2.8 %copy-start.3 = (bf16[1024,768]{1,0:T(8,128)(2,1)}, bf16[1024,768]{1,0:T(8,128)(2,1)S(1)}, u32[]{:S(2)}) copy-start(bf16[1024,768]{1,0:T(8,128)(2,1)S(1)} %get-tuple-element.136.dq_ref) | copy-start | bytes 4718596
  109.4 2.8 %copy-start.5 = (bf16[1024,768]{1,0:T(8,128)(2,1)}, bf16[1024,768]{1,0:T(8,128)(2,1)S(1)}, u32[]{:S(2)}) copy-start(bf16[1024,768]{1,0:T(8,128)(2,1)S(1)} %get-tuple-element.141.o_ref) | copy-start | bytes 4718596
  109.5 8.5 %collective-permute-start.5 = (bf16[128,512]{1,0:T(8,128)(2,1)S(1)}, bf16[128,512]{1,0:T(8,128)(2,1)S(1)}, u32[]{:S(2)}, u32[]{:S(2)}) collective-permute-start(bf16[128,512]{1,0:T(8,128)(2,1)S(1)} %get-tuple-element.140), channel_id=1, source_target_pairs={{0,1},{1,0},{2,3},{3,2},{4,5},{5,4},{6,7},{7,6},{8,9},{9,8},{10,11... | collective-permute-start | bytes 393224 | tf_op jit(solution)/shard_map/ppermute | solution.py:506
  111.1 2.1 %copy-start.4 = (bf16[768,1024]{1,0:T(8,128)(2,1)S(1)}, bf16[768,1024]{1,0:T(8,128)(2,1)}, u32[]{:S(2)}) copy-start(bf16[768,1024]{1,0:T(8,128)(2,1)} %get-tuple-element.142.ai_ref) | copy-start | bytes 4718596
  113.2 4.8 %copy-start.6 = (f32[1024,256]{1,0:T(8,128)S(1)}, f32[1024,256]{1,0:T(8,128)}, u32[]{:S(2)}) copy-start(f32[1024,256]{1,0:T(8,128)} %get-tuple-element.122.tab_ref) | copy-start | bytes 3145732
  120.3 3.2 %collective-permute-start.6 = (bf16[4,96,1664]{2,1,0:T(8,128)(2,1)}, bf16[4,96,1664]{2,1,0:T(8,128)(2,1)S(1)}, u32[]{:S(2)}, u32[]{:S(2)}) collective-permute-start(bf16[4,96,1664]{2,1,0:T(8,128)(2,1)} %get-tuple-element.153), channel_id=1, source_target_pairs={{0,4},{4,0},{8,12},{12,8},{16,20},{20,16},{24,28},{28,24},{1,5},{5... | collective-permute-start | bytes 3833864 | tf_op jit(solution)/shard_map/ppermute | solution.py:443
  123.9 16.1 %collective-permute-start.7 = (bf16[4,48,1664]{2,1,0:T(8,128)(2,1)S(1)}, bf16[4,48,1664]{2,1,0:T(8,128)(2,1)S(1)}, u32[]{:S(2)}, u32[]{:S(2)}) collective-permute-start(bf16[4,48,1664]{2,1,0:T(8,128)(2,1)S(1)} %get-tuple-element.197), channel_id=1, source_target_pairs={{0,8},{4,20},{8,0},{12,28},{16,24},{20,4},{24,16},{28,12},{1,9},{5... | collective-permute-start | bytes 1916936 | tf_op jit(solution)/shard_map/ppermute | solution.py:443
  124.6 15.4 %collective-permute-start.8 = (bf16[2,192,768]{2,1,0:T(8,128)(2,1)S(1)}, bf16[2,192,768]{2,1,0:T(8,128)(2,1)S(1)}, u32[]{:S(2)}, u32[]{:S(2)}) collective-permute-start(bf16[2,192,768]{2,1,0:T(8,128)(2,1)S(1)} %copy-done.11), channel_id=1, source_target_pairs={{0,1},{1,0},{2,3},{3,2},{4,5},{5,4},{6,7},{7,6},{8,9},{9,8},{10,11... | collective-permute-start | bytes 1769480 | tf_op jit(solution)/shard_map/ppermute | solution.py:443
  133.7 1.7 copy-start.1
  140.0 4.0 %copy-start.7 = (f32[12,768]{1,0:T(8,128)S(1)}, f32[12,768]{1,0:T(8,128)}, u32[]{:S(2)}) copy-start(f32[12,768]{1,0:T(8,128)} %table.1.refs_7_.vec_ref) | copy-start | bytes 110596
  140.0 4.0 %copy-start.9 = (f32[4,768]{1,0:T(4,128)S(1)}, f32[4,768]{1,0:T(4,128)}, u32[]{:S(2)}) copy-start(f32[4,768]{1,0:T(4,128)} %get-tuple-element.116.hb_ref) | copy-start | bytes 36868
  140.2 12.4 %collective-permute-start.9 = (bf16[4,24,1664]{2,1,0:T(8,128)(2,1)S(1)}, bf16[4,24,1664]{2,1,0:T(8,128)(2,1)S(1)}, u32[]{:S(2)}, u32[]{:S(2)}) collective-permute-start(bf16[4,24,1664]{2,1,0:T(8,128)(2,1)S(1)} %get-tuple-element.201), channel_id=1, source_target_pairs={{0,16},{4,12},{8,24},{12,4},{16,0},{20,28},{24,8},{28,20},{1,17},{... | collective-permute-start | bytes 958472 | tf_op jit(solution)/shard_map/ppermute | solution.py:443
  141.4 22.0 %collective-permute-start.11 = (bf16[192,768]{1,0:T(8,128)(2,1)S(1)}, bf16[192,768]{1,0:T(8,128)(2,1)S(1)}, u32[]{:S(2)}, u32[]{:S(2)}) collective-permute-start(bf16[192,768]{1,0:T(8,128)(2,1)S(1)} %fusion.7), channel_id=1, source_target_pairs={{0,2},{1,3},{2,0},{3,1},{4,6},{5,7},{6,4},{7,5},{8,10},{9,11},{10,... | collective-permute-start | bytes 884744 | tf_op jit(solution)/shard_map/ppermute | solution.py:443
  152.6 10.8 %collective-permute-start.12 = (f32[16,768]{1,0:T(8,128)S(1)}, f32[16,768]{1,0:T(8,128)S(1)}, u32[]{:S(2)}, u32[]{:S(2)}) collective-permute-start(f32[16,768]{1,0:T(8,128)S(1)} %get-tuple-element.163), channel_id=1, source_target_pairs={{0,4},{4,0},{8,12},{12,8},{16,20},{20,16},{24,28},{28,24},{1,5},{5... | collective-permute-start | bytes 147464 | tf_op jit(solution)/shard_map/ppermute | solution.py:537
  152.7 10.7 %collective-permute-start.10 = (bf16[2,24,1664]{2,1,0:T(8,128)(2,1)S(1)}, bf16[2,24,1664]{2,1,0:T(8,128)(2,1)S(1)}, u32[]{:S(2)}, u32[]{:S(2)}) collective-permute-start(bf16[2,24,1664]{2,1,0:T(8,128)(2,1)S(1)} %get-tuple-element.203), channel_id=1, source_target_pairs={{0,1},{1,0},{2,3},{3,2},{4,5},{5,4},{6,7},{7,6},{8,9},{9,8},{10,11... | collective-permute-start | bytes 479240 | tf_op jit(solution)/shard_map/ppermute | solution.py:443
  163.5 8.2 %collective-permute-start.14 = (bf16[192,768]{1,0:T(8,128)(2,1)S(1)}, bf16[192,768]{1,0:T(8,128)(2,1)S(1)}, u32[]{:S(2)}, u32[]{:S(2)}) collective-permute-start(bf16[192,768]{1,0:T(8,128)(2,1)S(1)} %fusion.3), channel_id=1, source_target_pairs={{0,16},{4,12},{8,24},{12,4},{16,0},{20,28},{24,8},{28,20},{1,17},{... | collective-permute-start | bytes 884744 | tf_op jit(solution)/shard_map/ppermute | solution.py:462
  164.6 6.9 %collective-permute-start.15 = (f32[16,768]{1,0:T(8,128)S(1)}, f32[16,768]{1,0:T(8,128)S(1)}, u32[]{:S(2)}, u32[]{:S(2)}) collective-permute-start(f32[16,768]{1,0:T(8,128)S(1)} %add.158), channel_id=1, source_target_pairs={{0,8},{4,20},{8,0},{12,28},{16,24},{20,4},{24,16},{28,12},{1,9},{5... | collective-permute-start | bytes 147464 | tf_op jit(solution)/shard_map/ppermute | solution.py:537
  165.1 6.6 %collective-permute-start.13 = (bf16[24,1664]{1,0:T(8,128)(2,1)S(1)}, bf16[24,1664]{1,0:T(8,128)(2,1)S(1)}, u32[]{:S(2)}, u32[]{:S(2)}) collective-permute-start(bf16[24,1664]{1,0:T(8,128)(2,1)S(1)} %fusion.13), channel_id=1, source_target_pairs={{0,2},{1,3},{2,0},{3,1},{4,6},{5,7},{6,4},{7,5},{8,10},{9,11},{10,... | collective-permute-start | bytes 239624 | tf_op jit(solution)/shard_map/ppermute | solution.py:443
  171.8 13.4 %collective-permute-start.19 = (bf16[384,768]{1,0:T(8,128)(2,1)S(1)}, bf16[384,768]{1,0:T(8,128)(2,1)S(1)}, u32[]{:S(2)}, u32[]{:S(2)}) collective-permute-start(bf16[384,768]{1,0:T(8,128)(2,1)S(1)} %pad_maximum_fusion.1), channel_id=1, source_target_pairs={{0,8},{4,20},{8,0},{12,28},{16,24},{20,4},{24,16},{28,12},{1,9},{5... | collective-permute-start | bytes 1769480 | tf_op jit(solution)/shard_map/ppermute | solution.py:462
  173.4 6.5 %collective-permute-start.16 = (bf16[24,1664]{1,0:T(8,128)(2,1)S(1)}, bf16[24,1664]{1,0:T(8,128)(2,1)S(1)}, u32[]{:S(2)}, u32[]{:S(2)}) collective-permute-start(bf16[24,1664]{1,0:T(8,128)(2,1)S(1)} %fusion.10), channel_id=1, source_target_pairs={{0,16},{4,12},{8,24},{12,4},{16,0},{20,28},{24,8},{28,20},{1,17},{... | collective-permute-start | bytes 239624 | tf_op jit(solution)/shard_map/ppermute | solution.py:462
  174.5 5.4 %collective-permute-start.17 = (f32[16,768]{1,0:T(8,128)S(1)}, f32[16,768]{1,0:T(8,128)S(1)}, u32[]{:S(2)}, u32[]{:S(2)}) collective-permute-start(f32[16,768]{1,0:T(8,128)S(1)} %add.161), channel_id=1, source_target_pairs={{0,16},{4,12},{8,24},{12,4},{16,0},{20,28},{24,8},{28,20},{1,17},{... | collective-permute-start | bytes 147464 | tf_op jit(solution)/shard_map/ppermute | solution.py:537
  179.9 5.3 %collective-permute-start.18 = (bf16[48,1664]{1,0:T(8,128)(2,1)S(1)}, bf16[48,1664]{1,0:T(8,128)(2,1)S(1)}, u32[]{:S(2)}, u32[]{:S(2)}) collective-permute-start(bf16[48,1664]{1,0:T(8,128)(2,1)S(1)} %pad_maximum_fusion.3), channel_id=1, source_target_pairs={{0,8},{4,20},{8,0},{12,28},{16,24},{20,4},{24,16},{28,12},{1,9},{5... | collective-permute-start | bytes 479240 | tf_op jit(solution)/shard_map/ppermute | solution.py:462
  180.5 4.1 %collective-permute-start.20 = (f32[16,768]{1,0:T(8,128)S(1)}, f32[16,768]{1,0:T(8,128)S(1)}, u32[]{:S(2)}, u32[]{:S(2)}) collective-permute-start(f32[16,768]{1,0:T(8,128)S(1)} %add.162), channel_id=1, source_target_pairs={{0,1},{1,0},{2,3},{3,2},{4,5},{5,4},{6,7},{7,6},{8,9},{9,8},{10,11... | collective-permute-start | bytes 147464 | tf_op jit(solution)/shard_map/ppermute | solution.py:537
  185.3 6.4 %collective-permute-start.21 = (bf16[768,768]{1,0:T(8,128)(2,1)S(1)}, bf16[768,768]{1,0:T(8,128)(2,1)S(1)}, u32[]{:S(2)}, u32[]{:S(2)}) collective-permute-start(bf16[768,768]{1,0:T(8,128)(2,1)S(1)} %pad_maximum_fusion.m_ref), channel_id=1, source_target_pairs={{0,4},{4,0},{8,12},{12,8},{16,20},{20,16},{24,28},{28,24},{1,5},{5... | collective-permute-start | bytes 3538952 | tf_op jit(solution)/shard_map/ppermute | solution.py:560
  185.5 6.3 %collective-permute-start.22 = (bf16[96,1664]{1,0:T(8,128)(2,1)S(1)}, bf16[96,1664]{1,0:T(8,128)(2,1)S(1)}, u32[]{:S(2)}, u32[]{:S(2)}) collective-permute-start(bf16[96,1664]{1,0:T(8,128)(2,1)S(1)} %pad_maximum_fusion.2.a_ref), channel_id=1, source_target_pairs={{0,4},{4,0},{8,12},{12,8},{16,20},{20,16},{24,28},{28,24},{1,5},{5... | collective-permute-start | bytes 958472 | tf_op jit(solution)/shard_map/ppermute | solution.py:561
  186.0 5.7 %collective-permute-start.23 = (f32[16,768]{1,0:T(8,128)S(1)}, f32[16,768]{1,0:T(8,128)S(1)}, u32[]{:S(2)}, u32[]{:S(2)}) collective-permute-start(f32[16,768]{1,0:T(8,128)S(1)} %add.163.s_ref), channel_id=1, source_target_pairs={{0,2},{1,3},{2,0},{3,1},{4,6},{5,7},{6,4},{7,5},{8,10},{9,11},{10,... | collective-permute-start | bytes 147464 | tf_op jit(solution)/shard_map/ppermute | solution.py:563
  (4 other events, 5.0 us)
